TPU v7x, 256 devices: a whole 4x4x8 slice. The times are simulated.
256 devices in a mesh: role: 4 (over y), gx: 16 (over z, core), gz: 4 (over x).
Axes of the slice: x: 4, y: 4, z: 8, core: 2. Of those that a mesh axis runs over, the one named last changes fastest.
Arguments:
- pressure_old: float32 [64, 1024, 512], P('gz', 'gx', 'role'), may hold values from -2.5 to -0.2
- vg_alpha: float32 [64, 1024, 512], P('gz', 'gx', 'role'), may hold values from 0.5 to 1.5
- vg_n: float32 [64, 1024, 512], P('gz', 'gx', 'role'), may hold values from 1.3 to 2.5
- conductivity_sat: float32 [64, 1024, 512], P('gz', 'gx', 'role'), may hold values from 0.05 to 1
- porosity: float32 [64, 1024, 512], P('gz', 'gx', 'role'), may hold values from 0.25 to 0.45
- tile_owner: int32 [1024, 4], replicated, may hold values from -1 to 63, as said below
- land_temp: float32 [4, 64, 48, 16, 128], P('role', ('gx', 'gz')), may hold values from -6 to 6
- transpiration: float32 [4, 64, 48, 128], P('role', ('gx', 'gz')), may hold values from 0.2 to 1
- air_temp: float32 [4, 64, 48, 128], P('role', ('gx', 'gz')), may hold values from -6 to 6
- root_layers: int32 [4, 64, 48, 128], P('role', ('gx', 'gz')), may hold values from 1 to 16
Outputs:
- pressure_new: float32 [64, 1024, 512], P('gz', 'gx', 'role')
- land_temp_new: float32 [4, 64, 48, 16, 128], P('role', ('gx', 'gz'))
Inputs may be any that keep to these rules, and one draw needn't show every extreme that they name: `tile_owner`: -1 marks an inactive tile; otherwise the value is the land device, numbered along gx and gz with gz fastest, within the tile's role group; at most 3 tiles of one block have the same owner, and in every block one owner holds exactly 3 of them.
All inputs are finite; a program needn't handle non-finite values.
Results may differ from a plain program's by a relative error of at most 0.00002.
Values sent between devices are 32-bit elements; how exact they have to be, the bound alone decides.
A program may use at most 64 MiB of HBM per device.

v0:
```python
import math

import jax
import jax.numpy as jnp
from jax import lax
from jax.sharding import PartitionSpec as P

LAYERS = 16
LEVELS_PER_LAYER = 4
CAP = 3
SWEEPS = 3
HEAT_STEPS = 4


def with_halo(cells, sides, width):
    for axis, dim in sides:
        count = lax.axis_size(axis)
        ends = count - 1
        head = lax.slice_in_dim(cells, 0, width, axis=dim)
        tail = lax.slice_in_dim(cells, cells.shape[dim] - width, cells.shape[dim], axis=dim)
        cells = jnp.concatenate(
            [
                lax.ppermute(tail, axis, [(i, (i + 1) % count) for i in range(ends)]),
                cells,
                lax.ppermute(head, axis, [((i + 1) % count, i) for i in range(ends)]),
            ],
            axis=dim,
        )
    return cells


def soil_curves(head, alpha, vgn, ksat):
    suction = jnp.sqrt(head * head + 0.01)
    logx = vgn * jnp.log(alpha * suction)
    expo = 1.0 - 1.0 / vgn
    softer = jnp.log1p(jnp.exp(logx))
    satur = jnp.exp(-expo * softer)
    cond = ksat * jnp.sqrt(satur) * (1.0 - jnp.exp(expo * (logx - softer))) ** 2
    return (satur, cond)


def layer_mean(values, axis):
    shape = values.shape
    split = shape[:axis] + (shape[axis] // 4, 4) + shape[axis + 1 :]
    parts = values.reshape(split)
    first = lax.index_in_dim(parts, 0, axis + 1, keepdims=False)
    second = lax.index_in_dim(parts, 1, axis + 1, keepdims=False)
    third = lax.index_in_dim(parts, 2, axis + 1, keepdims=False)
    fourth = lax.index_in_dim(parts, 3, axis + 1, keepdims=False)
    return (first + second + third + fourth) * 0.25


def land_step(satur, head, temps, tpot, air, roots):
    nlayer = satur.shape[-2]
    layer = jnp.arange(nlayer, dtype=jnp.float32)[:, None]
    depth = jnp.arange(nlayer, dtype=jnp.int32)[:, None]
    weights = jnp.exp(-layer / 4.0) * (depth < roots[..., None, :]).astype(jnp.float32)
    weights = weights / jnp.sum(weights, axis=-2, keepdims=True)
    stress = 1.0 / (1.0 + head * head / 2.25)
    uptake = tpot[..., None, :] * weights * stress
    kappa = 0.25 + 0.9 * satur
    inner = 0.5 * (kappa[..., :-1, :] + kappa[..., 1:, :])
    k_above = jnp.concatenate([kappa[..., :1, :], inner], axis=-2)
    k_below = jnp.concatenate([inner, jnp.zeros_like(kappa[..., :1, :])], axis=-2)
    for substep in range(HEAT_STEPS):
        above = jnp.concatenate([air[..., None, :], temps[..., :-1, :]], axis=-2)
        below = jnp.concatenate([temps[..., 1:, :], temps[..., -1:, :]], axis=-2)
        temps = temps + 0.2 * (k_above * (above - temps) + k_below * (below - temps)) - 0.3 * uptake
    return (uptake, temps)


def sweep_update(padh, padk, masks, head, cond, water, theta_old, sink, omega):
    mask_up, mask_down, mask_xm, mask_xp, mask_ym, mask_yp = masks
    near_up = padh[:-2, 1:-1, 1:-1]
    near_down = padh[2:, 1:-1, 1:-1]
    near_xm = padh[1:-1, :-2, 1:-1]
    near_xp = padh[1:-1, 2:, 1:-1]
    near_ym = padh[1:-1, 1:-1, :-2]
    near_yp = padh[1:-1, 1:-1, 2:]
    kf_up = 0.5 * (cond + padk[:-2, 1:-1, 1:-1]) * mask_up
    kf_down = 0.5 * (cond + padk[2:, 1:-1, 1:-1]) * mask_down
    kf_xm = 0.5 * (cond + padk[1:-1, :-2, 1:-1]) * mask_xm
    kf_xp = 0.5 * (cond + padk[1:-1, 2:, 1:-1]) * mask_xp
    kf_ym = 0.5 * (cond + padk[1:-1, 1:-1, :-2]) * mask_ym
    kf_yp = 0.5 * (cond + padk[1:-1, 1:-1, 2:]) * mask_yp
    flux = kf_up * (head - near_up) + kf_down * (head - near_down)
    flux = flux + kf_xm * (head - near_xm) + kf_xp * (head - near_xp)
    flux = flux + kf_ym * (head - near_ym) + kf_yp * (head - near_yp)
    resid = water - theta_old + flux + (kf_down - kf_up) + sink
    diag = 1.0 + (kf_up + kf_down + kf_xm + kf_xp + kf_ym + kf_yp)
    return head - omega * resid / diag


def local(
    pressure_old,
    vg_alpha,
    vg_n,
    conductivity_sat,
    porosity,
    tile_owner,
    land_temp,
    transpiration,
    air_temp,
    root_layers,
):
    levels, rows, columns = pressure_old.shape
    count_gx = lax.axis_size("gx")
    count_gz = lax.axis_size("gz")
    groups = count_gx * count_gz
    total_levels = levels * count_gz
    total_rows = rows * count_gx
    total_columns = columns * lax.axis_size("role")
    local_layers = levels // LEVELS_PER_LAYER
    index_gx = lax.axis_index("gx")
    index_gz = lax.axis_index("gz")
    index_role = lax.axis_index("role")
    satur_old, cond_old = soil_curves(pressure_old, vg_alpha, vg_n, conductivity_sat)
    theta_old = porosity * satur_old
    owners = lax.dynamic_slice(tile_owner, (index_gx * rows, index_role), (rows, 1))[:, 0]
    same_owner = owners[:, None] == owners[None, :]
    earlier = jnp.arange(rows)[:, None] > jnp.arange(rows)[None, :]
    rank = jnp.sum((same_owner & earlier).astype(jnp.int32), axis=1)
    active = owners >= 0
    flat_slot = jnp.where(active, owners * CAP + rank, groups * CAP)
    payload = jnp.stack([satur_old, pressure_old]).transpose(2, 0, 1, 3)
    outgoing = (
        jnp.zeros((groups * CAP,) + payload.shape[1:], jnp.float32)
        .at[flat_slot]
        .set(payload, mode="drop")
    )
    received = lax.all_to_all(
        outgoing.reshape((groups, CAP) + payload.shape[1:]),
        ("gx", "gz"),
        split_axis=0,
        concat_axis=0,
        tiled=True,
    )
    received = received.reshape((count_gx, count_gz, CAP) + payload.shape[1:])
    received = layer_mean(received, 4)
    gathered = received.transpose(0, 2, 3, 1, 4, 5).reshape(count_gx * CAP, 2, LAYERS, columns)
    temps = land_temp[0, 0]
    uptake, new_temps = land_step(
        gathered[:, 0],
        gathered[:, 1],
        temps,
        transpiration[0, 0],
        air_temp[0, 0],
        root_layers[0, 0],
    )
    my_owner = index_gx * count_gz + index_gz
    role_owners = lax.dynamic_slice(tile_owner, (0, index_role), (total_rows, 1))[:, 0].reshape(
        count_gx, rows
    )
    counts = jnp.sum((role_owners == my_owner).astype(jnp.int32), axis=1)
    slot_index = jnp.arange(count_gx * CAP, dtype=jnp.int32)
    filled = slot_index % CAP < jnp.repeat(counts, CAP)
    land_temp_new = jnp.where(filled[:, None, None], new_temps, temps)[None, None]
    returning = uptake.reshape(count_gx, CAP, count_gz, local_layers, columns).transpose(
        0, 2, 1, 3, 4
    )
    came_back = lax.all_to_all(
        returning.reshape(groups, CAP, local_layers, columns),
        ("gx", "gz"),
        split_axis=0,
        concat_axis=0,
        tiled=True,
    )
    came_back = came_back.reshape(groups * CAP, local_layers, columns)
    tile_uptake = (
        came_back[jnp.clip(flat_slot, 0, groups * CAP - 1)]
        * active.astype(jnp.float32)[:, None, None]
    )
    sink = jnp.repeat(tile_uptake, LEVELS_PER_LAYER, axis=1).transpose(1, 0, 2)
    zglob = index_gz * levels + jnp.arange(levels)
    xglob = index_gx * rows + jnp.arange(rows)
    yglob = index_role * columns + jnp.arange(columns)
    masks = (
        (zglob > 0).astype(jnp.float32)[:, None, None],
        (zglob < total_levels - 1).astype(jnp.float32)[:, None, None],
        (xglob > 0).astype(jnp.float32)[None, :, None],
        (xglob < total_rows - 1).astype(jnp.float32)[None, :, None],
        (yglob > 0).astype(jnp.float32)[None, None, :],
        (yglob < total_columns - 1).astype(jnp.float32)[None, None, :],
    )
    head = pressure_old
    cond = cond_old
    water = theta_old
    for sweep_index in range(SWEEPS):
        if sweep_index > 0:
            satur, cond = soil_curves(head, vg_alpha, vg_n, conductivity_sat)
            water = porosity * satur
        omega = 1.0 / (1.0 + 0.6 * math.cos(math.pi * (2 * sweep_index + 1) / (2 * SWEEPS)))
        padded = with_halo(jnp.stack([head, cond]), (("role", 3), ("gx", 2), ("gz", 1)), 1)
        head = sweep_update(padded[0], padded[1], masks, head, cond, water, theta_old, sink, omega)
    return (head, land_temp_new)


def solution(mesh):
    in_specs = (
        P("gz", "gx", "role"),
        P("gz", "gx", "role"),
        P("gz", "gx", "role"),
        P("gz", "gx", "role"),
        P("gz", "gx", "role"),
        P(),
        P("role", ("gx", "gz"), None, None, None),
        P("role", ("gx", "gz"), None, None),
        P("role", ("gx", "gz"), None, None),
        P("role", ("gx", "gz"), None, None),
    )
    out_specs = (P("gz", "gx", "role"), P("role", ("gx", "gz"), None, None, None))
    return jax.shard_map(local, mesh=mesh, in_specs=in_specs, out_specs=out_specs, check_vma=False)
```

profile of v0, /device:TPU:1, one launch (start us, length us, event | category | flops | bytes accessed | tf_op | source)
XLA Modules:
  0.0 240.4 jit_solution(15636610479721688563)
XLA Ops:
  6.8 8.4 %scatter_fusion = f32[192,2,16,128]{3,2,1,0:T(8,128)} fusion(f32[192,2,16,128]{3,2,1,0:T(8,128)} %broadcast_in_dim.20, s32[64]{0:T(128)S(1)} %fusion.110, f32[64,2,16,128]{3,2,1,0:T(8,128)S(1)} %copy.168), kind=kCustom, calls=%fused_computation.1 | custom fusion | bytes 3145984 | tf_op jit(solution)/shard_map/scatter | solution.py:129
  15.2 13.3 %all-to-all-start = ((f32[64,3,2,16,128]{4,3,2,1,0:T(8,128)}), f32[64,3,2,16,128]{4,3,2,1,0:T(8,128)}, u32[]{:S(2)}, u32[]{:S(2)}) async-start(f32[64,3,2,16,128]{4,3,2,1,0:T(8,128)} %bitcast.109), calls=%async_computation | async-start | bytes 6291456 | tf_op jit(solution)/shard_map/all_to_all | solution.py:131
  30.6 3.0 %collective-permute-start = (f32[2,16,64,1]{2,1,3,0:T(8,128)S(1)}, f32[2,16,64,1]{2,1,3,0:T(8,128)S(1)}, u32[]{:S(2)}, u32[]{:S(2)}) collective-permute-start(f32[2,16,64,1]{2,1,3,0:T(8,128)S(1)} %copy.157), channel_id=1, source_target_pairs={{0,64},{64,128},{128,192},{1,65},{65,129},{129,193},{2,66},{66,130... | collective-permute-start | bytes 24584 | tf_op jit(solution)/shard_map/ppermute | solution.py:23
  40.4 4.7 %collective-permute-start.2 = (f32[2,16,1,130]{3,1,2,0:T(8,128)S(1)}, f32[2,16,1,130]{3,1,2,0:T(8,128)S(1)}, u32[]{:S(2)}, u32[]{:S(2)}) collective-permute-start(f32[2,16,1,130]{3,1,2,0:T(8,128)S(1)} %copy.161), channel_id=1, source_target_pairs={{0,4},{4,8},{8,12},{12,16},{16,20},{20,24},{24,28},{28,32},{32,36}... | collective-permute-start | bytes 49928 | tf_op jit(solution)/shard_map/ppermute | solution.py:23
  48.7 45.2 %collective-permute-done.2 = f32[2,16,1,130]{3,1,2,0:T(8,128)S(1)} collective-permute-done((f32[2,16,1,130]{3,1,2,0:T(8,128)S(1)}, f32[2,16,1,130]{3,1,2,0:T(8,128)S(1)}, u32[]{:S(2)}, u32[]{:S(2)}) %collective-permute-start.2) | collective-permute-done | bytes 16672 | tf_op jit(solution)/shard_map/ppermute | solution.py:23
  93.9 4.3 %collective-permute-done.3 = f32[2,16,1,130]{3,1,2,0:T(8,128)S(1)} collective-permute-done((f32[2,16,1,130]{3,1,2,0:T(8,128)S(1)}, f32[2,16,1,130]{3,1,2,0:T(8,128)S(1)}, u32[]{:S(2)}, u32[]{:S(2)}) %collective-permute-start.3) | collective-permute-done | bytes 16672 | tf_op jit(solution)/shard_map/ppermute | solution.py:25
  99.2 3.1 %collective-permute-start.4 = (f32[2,1,66,130]{3,2,1,0:T(8,128)S(1)}, f32[2,1,66,130]{3,2,1,0:T(8,128)S(1)}, u32[]{:S(2)}, u32[]{:S(2)}) collective-permute-start(f32[2,1,66,130]{3,2,1,0:T(8,128)S(1)} %get-tuple-element.22), channel_id=1, source_target_pairs={{0,1},{1,2},{2,3},{4,5},{5,6},{6,7},{8,9},{9,10},{10,11},{12,13},{... | collective-permute-start | bytes 205928 | tf_op jit(solution)/shard_map/ppermute | solution.py:23
  104.4 3.8 %collective-permute-done.5 = f32[2,1,66,130]{3,2,1,0:T(8,128)S(1)} collective-permute-done((f32[2,1,66,130]{3,2,1,0:T(8,128)S(1)}, f32[2,1,66,130]{3,2,1,0:T(8,128)S(1)}, u32[]{:S(2)}, u32[]{:S(2)}) %collective-permute-start.5) | collective-permute-done | bytes 68672 | tf_op jit(solution)/shard_map/ppermute | solution.py:25
  108.2 2.6 %pad_maximum_fusion = f32[2,18,66,130]{3,2,1,0:T(8,128)} fusion(f32[2,1,66,130]{3,2,1,0:T(8,128)S(1)} %collective-permute-done.5, f32[2,16,1,130]{3,2,1,0:T(1,128)S(1)} %copy.164, f32[2,16,64,1]{3,2,1,0:T(8,128)S(1)} %copy.160, f32[1,16,64,128]{3,2,1,0:T(8,128)S(1)} %copy-done.11, f32[1,16,64,128]{3,2,1,0:T(8,128)S(1)} %bitcast.100, ...), kind=kLoop, calls=%fused_computation.2 | loop fusion | flops 2162160 | bytes 2471040 | tf_op jit(solution)/shard_map/concatenate | solution.py:21
  110.8 8.7 %fusion.117 = (f32[16,4,3,2,4,1,128]{6,5,4,3,2,1,0:T(1,128)S(1)}, f32[16,4,3,2,4,1,128]{6,5,4,3,2,1,0:T(1,128)S(1)}, f32[16,4,3,2,4,1,128]{6,5,4,3,2,1,0:T(1,128)S(1)}, f32[16,4,3,2,4,1,128]{6,5,4,3,2,1,0:T(1,128)S(1)}) fusion(f32[16,4,3,2,4,4,128]{6,5,4,3,2,1,0:T(4,128)} %bitcast.11), kind=kLoop, calls=%fused_computation.257 | loop fusion | bytes 6291456 | tf_op jit(solution)/shard_map/slice | solution.py:46
  122.1 11.1 %all-to-all-start.1 = ((f32[64,3,4,128]{3,2,1,0:T(4,128)}), f32[64,3,4,128]{3,2,1,0:T(4,128)}, u32[]{:S(2)}, u32[]{:S(2)}) async-start(f32[64,3,4,128]{3,2,1,0:T(4,128)} %copy.174), calls=%async_computation.1 | async-start | bytes 786432 | tf_op jit(solution)/shard_map/all_to_all | solution.py:161
  133.2 3.1 %slice_bitcast_fusion.5 = (f32[18,66,130]{2,1,0:T(8,128)S(1)}, f32[18,66,130]{2,1,0:T(8,128)}) fusion(f32[2,18,66,130]{3,2,1,0:T(8,128)} %pad_maximum_fusion), kind=kLoop, calls=%fused_computation.10 | loop fusion | bytes 2471040 | tf_op jit(solution)/shard_map/squeeze | solution.py:194
  138.9 8.8 %all-to-all-done.1 = f32[64,3,4,128]{3,2,1,0:T(4,128)} async-done(((f32[64,3,4,128]{3,2,1,0:T(4,128)}), f32[64,3,4,128]{3,2,1,0:T(4,128)}, u32[]{:S(2)}, u32[]{:S(2)}) %all-to-all-start.1) | async-done | bytes 393248 | tf_op jit(solution)/shard_map/all_to_all | solution.py:161
  149.6 6.6 %fusion.113 = (f32[1,16,64,128]{3,2,1,0:T(8,128)S(1)}, f32[16,64,128]{2,1,0:T(8,128)S(1)}) fusion(f32[16,64,128]{2,1,0:T(8,128)} %param.13, f32[16,64,128]{2,1,0:T(8,128)S(1)} %copy-done.1, f32[16,64,128]{2,1,0:T(8,128)} %param.11, f32[16,64,128]{2,1,0:T(8,128)S(1)} %copy-done, f32[64,4,128]{2,0,1:T(8,128)S(1)} %copy_multiply_fusion.1, ...), kind=kLoop, calls=%fused_computation.255 | loop fusion | flops 8519680 | bytes 10618496 | tf_op jit(solution)/shard_map/stack | solution.py:193
  160.0 3.0 %collective-permute-start.6 = (f32[2,16,64,1]{2,1,3,0:T(8,128)S(1)}, f32[2,16,64,1]{2,1,3,0:T(8,128)S(1)}, u32[]{:S(2)}, u32[]{:S(2)}) collective-permute-start(f32[2,16,64,1]{2,1,3,0:T(8,128)S(1)} %copy.176), channel_id=1, source_target_pairs={{0,64},{64,128},{128,192},{1,65},{65,129},{129,193},{2,66},{66,130... | collective-permute-start | bytes 24584 | tf_op jit(solution)/shard_map/ppermute | solution.py:23
  171.4 5.9 %collective-permute-start.8 = (f32[2,16,1,130]{3,1,2,0:T(8,128)S(1)}, f32[2,16,1,130]{3,1,2,0:T(8,128)S(1)}, u32[]{:S(2)}, u32[]{:S(2)}) collective-permute-start(f32[2,16,1,130]{3,1,2,0:T(8,128)S(1)} %copy.180), channel_id=1, source_target_pairs={{0,4},{4,8},{8,12},{12,16},{16,20},{20,24},{24,28},{28,32},{32,36}... | collective-permute-start | bytes 49928 | tf_op jit(solution)/shard_map/ppermute | solution.py:23
  187.9 3.2 %collective-permute-done.11 = f32[2,1,66,130]{3,2,1,0:T(8,128)S(1)} collective-permute-done((f32[2,1,66,130]{3,2,1,0:T(8,128)S(1)}, f32[2,1,66,130]{3,2,1,0:T(8,128)S(1)}, u32[]{:S(2)}, u32[]{:S(2)}) %collective-permute-start.11) | collective-permute-done | bytes 68672 | tf_op jit(solution)/shard_map/ppermute | solution.py:25
  193.7 3.6 %fusion.114 = (f32[1,16,64,128]{3,2,1,0:T(8,128)S(1)}, f32[16,64,128]{2,1,0:T(8,128)S(1)}) fusion(f32[16,64,128]{2,1,0:T(8,128)S(1)} %copy-done.22, f32[16,64,128]{2,1,0:T(8,128)S(1)} %copy-done.2, f32[16,64,128]{2,1,0:T(8,128)S(1)} %copy-done.19, f32[16,64,128]{2,1,0:T(8,128)S(1)} %get-tuple-element.11, f32[64,4,128]{2,0,1:T(8,128)S(1)} %copy-done.35, ...), kind=kLoop, calls=%fused_computation.256 | loop fusion | flops 9175040 | bytes 10618496 | tf_op jit(solution)/shard_map/stack | solution.py:193
  201.4 4.0 %collective-permute-start.12 = (f32[2,16,64,1]{2,1,3,0:T(8,128)S(1)}, f32[2,16,64,1]{2,1,3,0:T(8,128)}, u32[]{:S(2)}, u32[]{:S(2)}) collective-permute-start(f32[2,16,64,1]{2,1,3,0:T(8,128)S(1)} %copy.184), channel_id=1, source_target_pairs={{0,64},{64,128},{128,192},{1,65},{65,129},{129,193},{2,66},{66,130... | collective-permute-start | bytes 24584 | tf_op jit(solution)/shard_map/ppermute | solution.py:23
  215.2 4.6 %collective-permute-start.14 = (f32[2,16,1,130]{3,1,2,0:T(8,128)S(1)}, f32[2,16,1,130]{3,1,2,0:T(8,128)S(1)}, u32[]{:S(2)}, u32[]{:S(2)}) collective-permute-start(f32[2,16,1,130]{3,1,2,0:T(8,128)S(1)} %copy.188), channel_id=1, source_target_pairs={{0,4},{4,8},{8,12},{12,16},{16,20},{20,24},{24,28},{28,32},{32,36}... | collective-permute-start | bytes 49928 | tf_op jit(solution)/shard_map/ppermute | solution.py:23
  222.1 3.1 %collective-permute-done.15 = f32[2,16,1,130]{3,1,2,0:T(8,128)S(1)} collective-permute-done((f32[2,16,1,130]{3,1,2,0:T(8,128)S(1)}, f32[2,16,1,130]{3,1,2,0:T(8,128)S(1)}, u32[]{:S(2)}, u32[]{:S(2)}) %collective-permute-start.15) | collective-permute-done | bytes 16672 | tf_op jit(solution)/shard_map/ppermute | solution.py:25
  225.5 2.6 %collective-permute-start.16 = (f32[2,1,66,130]{3,2,1,0:T(8,128)S(1)}, f32[2,1,66,130]{3,2,1,0:T(8,128)S(1)}, u32[]{:S(2)}, u32[]{:S(2)}) collective-permute-start(f32[2,1,66,130]{3,2,1,0:T(8,128)S(1)} %get-tuple-element.18), channel_id=1, source_target_pairs={{0,1},{1,2},{2,3},{4,5},{5,6},{6,7},{8,9},{9,10},{10,11},{12,13},{... | collective-permute-start | bytes 205928 | tf_op jit(solution)/shard_map/ppermute | solution.py:23
  230.9 3.3 %collective-permute-done.17 = f32[2,1,66,130]{3,2,1,0:T(8,128)S(1)} collective-permute-done((f32[2,1,66,130]{3,2,1,0:T(8,128)S(1)}, f32[2,1,66,130]{3,2,1,0:T(8,128)S(1)}, u32[]{:S(2)}, u32[]{:S(2)}) %collective-permute-start.17) | collective-permute-done | bytes 68672 | tf_op jit(solution)/shard_map/ppermute | solution.py:25
  236.8 3.5 %fusion.8 = f32[16,64,128]{2,1,0:T(8,128)} fusion(f32[16,64,128]{2,1,0:T(8,128)S(1)} %get-tuple-element.9, f32[18,66,130]{2,1,0:T(8,128)S(1)} %get-tuple-element.35, f32[18,66,130]{2,1,0:T(8,128)S(1)} %get-tuple-element.34, f32[16,64,128]{2,1,0:T(8,128)S(1)} %copy-done.32, f32[64,4,128]{2,0,1:T(8,128)S(1)} %copy-done.36, f32[128]{0:T(128)S(1)} %copy-done.70, ...), kind=kLoop, calls=%fused_computation.36 | loop fusion | flops 7864320 | bytes 10094208 | tf_op jit(solution)/shard_map/sub | solution.py:91
  (266 shorter events, 74.7 us)
Async XLA Ops:
  4.1 24.4 %copy-start.3 = (f32[16,64,128]{2,1,0:T(8,128)}, f32[16,64,128]{2,1,0:T(8,128)S(1)}, u32[]{:S(2)}) copy-start(f32[16,64,128]{2,1,0:T(8,128)S(1)} %get-tuple-element.17) | copy-start | bytes 1572868
  15.2 95.6 %all-to-all-start = ((f32[64,3,2,16,128]{4,3,2,1,0:T(8,128)}), f32[64,3,2,16,128]{4,3,2,1,0:T(8,128)}, u32[]{:S(2)}, u32[]{:S(2)}) async-start(f32[64,3,2,16,128]{4,3,2,1,0:T(8,128)} %bitcast.109), calls=%async_computation | async-start | bytes 6291456 | tf_op jit(solution)/shard_map/all_to_all | solution.py:131
  30.6 7.8 %collective-permute-start = (f32[2,16,64,1]{2,1,3,0:T(8,128)S(1)}, f32[2,16,64,1]{2,1,3,0:T(8,128)S(1)}, u32[]{:S(2)}, u32[]{:S(2)}) collective-permute-start(f32[2,16,64,1]{2,1,3,0:T(8,128)S(1)} %copy.157), channel_id=1, source_target_pairs={{0,64},{64,128},{128,192},{1,65},{65,129},{129,193},{2,66},{66,130... | collective-permute-start | bytes 24584 | tf_op jit(solution)/shard_map/ppermute | solution.py:23
  34.0 4.8 %collective-permute-start.1 = (f32[2,16,64,1]{2,1,3,0:T(8,128)S(1)}, f32[2,16,64,1]{2,1,3,0:T(8,128)S(1)}, u32[]{:S(2)}, u32[]{:S(2)}) collective-permute-start(f32[2,16,64,1]{2,1,3,0:T(8,128)S(1)} %copy.158), channel_id=1, source_target_pairs={{64,0},{128,64},{192,128},{65,1},{129,65},{193,129},{66,2},{130,66... | collective-permute-start | bytes 24584 | tf_op jit(solution)/shard_map/ppermute | solution.py:25
  36.5 101.2 %copy-start.62 = (f32[16]{0:T(128)}, f32[16]{0:T(128)S(1)}, u32[]{:S(2)}) copy-start(f32[16]{0:T(128)S(1)} %multiply_exponential_fusion.4) | copy-start | bytes 196
  37.3 100.4 %copy-start.45 = (f32[48,128]{1,0:T(8,128)}, f32[48,128]{1,0:T(8,128)S(1)}, u32[]{:S(2)}) copy-start(f32[48,128]{1,0:T(8,128)S(1)} %select_reduce_fusion) | copy-start | bytes 73732
  40.4 53.5 %collective-permute-start.2 = (f32[2,16,1,130]{3,1,2,0:T(8,128)S(1)}, f32[2,16,1,130]{3,1,2,0:T(8,128)S(1)}, u32[]{:S(2)}, u32[]{:S(2)}) collective-permute-start(f32[2,16,1,130]{3,1,2,0:T(8,128)S(1)} %copy.161), channel_id=1, source_target_pairs={{0,4},{4,8},{8,12},{12,16},{16,20},{20,24},{24,28},{28,32},{32,36}... | collective-permute-start | bytes 49928 | tf_op jit(solution)/shard_map/ppermute | solution.py:23
  45.1 53.1 %collective-permute-start.3 = (f32[2,16,1,130]{3,1,2,0:T(8,128)S(1)}, f32[2,16,1,130]{3,1,2,0:T(8,128)S(1)}, u32[]{:S(2)}, u32[]{:S(2)}) collective-permute-start(f32[2,16,1,130]{3,1,2,0:T(8,128)S(1)} %copy.162), channel_id=1, source_target_pairs={{4,0},{8,4},{12,8},{16,12},{20,16},{24,20},{28,24},{32,28},{36,32}... | collective-permute-start | bytes 49928 | tf_op jit(solution)/shard_map/ppermute | solution.py:25
  48.7 59.5 %copy-start.11 = (f32[1,16,64,128]{3,2,1,0:T(8,128)S(1)}, f32[1,16,64,128]{3,2,1,0:T(8,128)}, u32[]{:S(2)}) copy-start(f32[1,16,64,128]{3,2,1,0:T(8,128)} %copy-done.10) | copy-start | bytes 1572868
  99.2 5.2 %collective-permute-start.4 = (f32[2,1,66,130]{3,2,1,0:T(8,128)S(1)}, f32[2,1,66,130]{3,2,1,0:T(8,128)S(1)}, u32[]{:S(2)}, u32[]{:S(2)}) collective-permute-start(f32[2,1,66,130]{3,2,1,0:T(8,128)S(1)} %get-tuple-element.22), channel_id=1, source_target_pairs={{0,1},{1,2},{2,3},{4,5},{5,6},{6,7},{8,9},{9,10},{10,11},{12,13},{... | collective-permute-start | bytes 205928 | tf_op jit(solution)/shard_map/ppermute | solution.py:23
  102.3 5.9 %collective-permute-start.5 = (f32[2,1,66,130]{3,2,1,0:T(8,128)S(1)}, f32[2,1,66,130]{3,2,1,0:T(8,128)S(1)}, u32[]{:S(2)}, u32[]{:S(2)}) collective-permute-start(f32[2,1,66,130]{3,2,1,0:T(8,128)S(1)} %get-tuple-element.23), channel_id=1, source_target_pairs={{1,0},{2,1},{3,2},{5,4},{6,5},{7,6},{9,8},{10,9},{11,10},{13,12},{... | collective-permute-start | bytes 205928 | tf_op jit(solution)/shard_map/ppermute | solution.py:25
  122.1 25.7 %all-to-all-start.1 = ((f32[64,3,4,128]{3,2,1,0:T(4,128)}), f32[64,3,4,128]{3,2,1,0:T(4,128)}, u32[]{:S(2)}, u32[]{:S(2)}) async-start(f32[64,3,4,128]{3,2,1,0:T(4,128)} %copy.174), calls=%async_computation.1 | async-start | bytes 786432 | tf_op jit(solution)/shard_map/all_to_all | solution.py:161
  160.0 6.8 %collective-permute-start.6 = (f32[2,16,64,1]{2,1,3,0:T(8,128)S(1)}, f32[2,16,64,1]{2,1,3,0:T(8,128)S(1)}, u32[]{:S(2)}, u32[]{:S(2)}) collective-permute-start(f32[2,16,64,1]{2,1,3,0:T(8,128)S(1)} %copy.176), channel_id=1, source_target_pairs={{0,64},{64,128},{128,192},{1,65},{65,129},{129,193},{2,66},{66,130... | collective-permute-start | bytes 24584 | tf_op jit(solution)/shard_map/ppermute | solution.py:23
  164.0 4.8 %collective-permute-start.7 = (f32[2,16,64,1]{2,1,3,0:T(8,128)}, f32[2,16,64,1]{2,1,3,0:T(8,128)}, u32[]{:S(2)}, u32[]{:S(2)}) collective-permute-start(f32[2,16,64,1]{2,1,3,0:T(8,128)} %copy.177), channel_id=1, source_target_pairs={{64,0},{128,64},{192,128},{65,1},{129,65},{193,129},{66,2},{130,66... | collective-permute-start | bytes 24584 | tf_op jit(solution)/shard_map/ppermute | solution.py:25
  171.4 9.1 %collective-permute-start.8 = (f32[2,16,1,130]{3,1,2,0:T(8,128)S(1)}, f32[2,16,1,130]{3,1,2,0:T(8,128)S(1)}, u32[]{:S(2)}, u32[]{:S(2)}) collective-permute-start(f32[2,16,1,130]{3,1,2,0:T(8,128)S(1)} %copy.180), channel_id=1, source_target_pairs={{0,4},{4,8},{8,12},{12,16},{16,20},{20,24},{24,28},{28,32},{32,36}... | collective-permute-start | bytes 49928 | tf_op jit(solution)/shard_map/ppermute | solution.py:23
  177.3 5.2 %collective-permute-start.9 = (f32[2,16,1,130]{3,1,2,0:T(8,128)S(1)}, f32[2,16,1,130]{3,1,2,0:T(8,128)S(1)}, u32[]{:S(2)}, u32[]{:S(2)}) collective-permute-start(f32[2,16,1,130]{3,1,2,0:T(8,128)S(1)} %copy.181), channel_id=1, source_target_pairs={{4,0},{8,4},{12,8},{16,12},{20,16},{24,20},{28,24},{32,28},{36,32}... | collective-permute-start | bytes 49928 | tf_op jit(solution)/shard_map/ppermute | solution.py:25
  182.8 5.1 %collective-permute-start.10 = (f32[2,1,66,130]{3,2,1,0:T(8,128)S(1)}, f32[2,1,66,130]{3,2,1,0:T(8,128)S(1)}, u32[]{:S(2)}, u32[]{:S(2)}) collective-permute-start(f32[2,1,66,130]{3,2,1,0:T(8,128)S(1)} %get-tuple-element.20), channel_id=1, source_target_pairs={{0,1},{1,2},{2,3},{4,5},{5,6},{6,7},{8,9},{9,10},{10,11},{12,13},{... | collective-permute-start | bytes 205928 | tf_op jit(solution)/shard_map/ppermute | solution.py:23
  185.0 6.1 %collective-permute-start.11 = (f32[2,1,66,130]{3,2,1,0:T(8,128)S(1)}, f32[2,1,66,130]{3,2,1,0:T(8,128)S(1)}, u32[]{:S(2)}, u32[]{:S(2)}) collective-permute-start(f32[2,1,66,130]{3,2,1,0:T(8,128)S(1)} %get-tuple-element.21), channel_id=1, source_target_pairs={{1,0},{2,1},{3,2},{5,4},{6,5},{7,6},{9,8},{10,9},{11,10},{13,12},{... | collective-permute-start | bytes 205928 | tf_op jit(solution)/shard_map/ppermute | solution.py:25
  201.4 9.4 %collective-permute-start.12 = (f32[2,16,64,1]{2,1,3,0:T(8,128)S(1)}, f32[2,16,64,1]{2,1,3,0:T(8,128)}, u32[]{:S(2)}, u32[]{:S(2)}) collective-permute-start(f32[2,16,64,1]{2,1,3,0:T(8,128)S(1)} %copy.184), channel_id=1, source_target_pairs={{0,64},{64,128},{128,192},{1,65},{65,129},{129,193},{2,66},{66,130... | collective-permute-start | bytes 24584 | tf_op jit(solution)/shard_map/ppermute | solution.py:23
  207.6 5.3 %collective-permute-start.13 = (f32[2,16,64,1]{2,1,3,0:T(8,128)}, f32[2,16,64,1]{2,1,3,0:T(8,128)}, u32[]{:S(2)}, u32[]{:S(2)}) collective-permute-start(f32[2,16,64,1]{2,1,3,0:T(8,128)} %copy.185), channel_id=1, source_target_pairs={{64,0},{128,64},{192,128},{65,1},{129,65},{193,129},{66,2},{130,66... | collective-permute-start | bytes 24584 | tf_op jit(solution)/shard_map/ppermute | solution.py:25
  215.2 6.9 %collective-permute-start.14 = (f32[2,16,1,130]{3,1,2,0:T(8,128)S(1)}, f32[2,16,1,130]{3,1,2,0:T(8,128)S(1)}, u32[]{:S(2)}, u32[]{:S(2)}) collective-permute-start(f32[2,16,1,130]{3,1,2,0:T(8,128)S(1)} %copy.188), channel_id=1, source_target_pairs={{0,4},{4,8},{8,12},{12,16},{16,20},{20,24},{24,28},{28,32},{32,36}... | collective-permute-start | bytes 49928 | tf_op jit(solution)/shard_map/ppermute | solution.py:23
  219.9 5.4 %collective-permute-start.15 = (f32[2,16,1,130]{3,1,2,0:T(8,128)S(1)}, f32[2,16,1,130]{3,1,2,0:T(8,128)S(1)}, u32[]{:S(2)}, u32[]{:S(2)}) collective-permute-start(f32[2,16,1,130]{3,1,2,0:T(8,128)S(1)} %copy.189), channel_id=1, source_target_pairs={{4,0},{8,4},{12,8},{16,12},{20,16},{24,20},{28,24},{32,28},{36,32}... | collective-permute-start | bytes 49928 | tf_op jit(solution)/shard_map/ppermute | solution.py:25
  225.5 5.4 %collective-permute-start.16 = (f32[2,1,66,130]{3,2,1,0:T(8,128)S(1)}, f32[2,1,66,130]{3,2,1,0:T(8,128)S(1)}, u32[]{:S(2)}, u32[]{:S(2)}) collective-permute-start(f32[2,1,66,130]{3,2,1,0:T(8,128)S(1)} %get-tuple-element.18), channel_id=1, source_target_pairs={{0,1},{1,2},{2,3},{4,5},{5,6},{6,7},{8,9},{9,10},{10,11},{12,13},{... | collective-permute-start | bytes 205928 | tf_op jit(solution)/shard_map/ppermute | solution.py:23
  228.1 6.1 %collective-permute-start.17 = (f32[2,1,66,130]{3,2,1,0:T(8,128)S(1)}, f32[2,1,66,130]{3,2,1,0:T(8,128)S(1)}, u32[]{:S(2)}, u32[]{:S(2)}) collective-permute-start(f32[2,1,66,130]{3,2,1,0:T(8,128)S(1)} %get-tuple-element.19), channel_id=1, source_target_pairs={{1,0},{2,1},{3,2},{5,4},{6,5},{7,6},{9,8},{10,9},{11,10},{13,12},{... | collective-permute-start | bytes 205928 | tf_op jit(solution)/shard_map/ppermute | solution.py:25
  (75 other events, 518.6 us)
where the time goes:
time: 242 us; the launch traced here: 240 us
  waiting for transfers between devices  76.4 us (32%)
  starting transfers between devices  71.3 us (29%)
  local copies, waits for them, and re-layouts  48.1 us (20%)
  other arithmetic  42.3 us (17%)
    ppermute x9, waiting for transfers between devices, with_halo(): lax.ppermute(tail, axis, [(i, (i + 1) % count) for i in range(ends)])  45.4 us
    ppermute x9, starting transfers between devices, with_halo(): lax.ppermute(tail, axis, [(i, (i + 1) % count) for i in range(ends)])  33.1 us
    ppermute x9, waiting for transfers between devices, with_halo(): lax.ppermute(head, axis, [((i + 1) % count, i) for i in range(ends)])  22.2 us
    another operation x6, other arithmetic, local(): jnp.stack([head, cond])  14.2 us
    ppermute x9, starting transfers between devices, with_halo(): lax.ppermute(head, axis, [((i + 1) % count, i) for i in range(ends)])  13.8 us
    all_to_all x1, starting transfers between devices, local(): lax.all_to_all(outgoing.reshape((groups, CAP) + payload.shape[1:]), ('gx'...  13.3 us
    all_to_all x1, starting transfers between devices, local(): lax.all_to_all(returning.reshape(groups, CAP, local_layers, columns), ('g...  11.1 us
    all_to_all x1, waiting for transfers between devices, local(): lax.all_to_all(returning.reshape(groups, CAP, local_layers, columns), ('g...  8.82 us
  transfers between devices with their start and end apart: 20, of which 11 were waited for; matrix products, arithmetic and copies ran while one was open for 13% of the time, Pallas kernels for 0%

commit v1 on v0

v1 whole, which is shorter than its diff:
```python
import functools
import math

import jax
import jax.numpy as jnp
from jax import lax
from jax.experimental import pallas as pl
from jax.experimental.pallas import tpu as pltpu
from jax.sharding import PartitionSpec as P

LEVELS_PER_LAYER = 4
CAP = 3
SWEEPS = 3
HEAT_STEPS = 4
LOG2E = 1.0 / math.log(2.0)
CHUNK = 32
PAD = 8
MESH = pl.DeviceIdType.MESH
OMEGAS = [
    1.0 / (1.0 + 0.6 * math.cos(math.pi * (2 * k + 1) / (2 * SWEEPS))) for k in range(SWEEPS)
]


def curves(head, c1, c0, m, ks):
    lx = c1 * jnp.log(head * head + 0.01) + c0
    soft = jnp.log(1.0 + jnp.exp2(lx)) * LOG2E
    root = jnp.exp2(-0.5 * (m * soft))
    gap = 1.0 - jnp.exp2(m * (lx - soft))
    return root * root, ks * root * (gap * gap)


def split3(x):
    hi = x.astype(jnp.bfloat16)
    rest = x - hi.astype(jnp.float32)
    mid = rest.astype(jnp.bfloat16)
    return hi, mid, (rest - mid.astype(jnp.float32)).astype(jnp.bfloat16)


def kernel(
    n_role,
    n_gx,
    n_gz,
    p_hbm,
    al_hbm,
    vn_hbm,
    ks_hbm,
    po_hbm,
    own_hbm,
    lt_hbm,
    tr_hbm,
    ai_hbm,
    ro_hbm,
    out_p,
    out_lt,
    p_v,
    c0_v,
    c1_v,
    ks_v,
    po_v,
    m_v,
    th_v,
    ra_v,
    da_v,
    hp,
    kp,
    xs,
    xh,
    ys,
    yh,
    own_v,
    lt_v,
    tr_v,
    ai_v,
    ro_v,
    sel_v,
    get_v,
    act_v,
    cnt_v,
    tp_v,
    rt_v,
    tq_v,
    rq_v,
    sk_v,
    lh_v,
    mean_v,
    tx_v,
    rx_v,
    load_sem,
    zt_send,
    zt_recv,
    xt_send,
    xt_recv,
    h_send,
    h_recv,
    land_send,
    land_recv,
    line_sem,
):
    levels, rows, cols = p_hbm.shape
    layers = levels // LEVELS_PER_LAYER
    groups = n_gx * n_gz
    tile = 2 * layers
    per = CAP * tile
    role = lax.axis_index("role")
    gx = lax.axis_index("gx")
    gz = lax.axis_index("gz")
    me = gx * n_gz + gz

    barrier = pltpu.get_barrier_semaphore()

    def greet_gx(i, c):
        pl.semaphore_signal(
            barrier, inc=1, device_id={"gx": lax.rem(gx + i, n_gx)}, device_id_type=MESH
        )
        return c

    def greet_gz(i, c):
        pl.semaphore_signal(
            barrier, inc=1, device_id={"gz": lax.rem(gz + i, n_gz)}, device_id_type=MESH
        )
        return c

    lax.fori_loop(1, n_gx, greet_gx, 0)
    lax.fori_loop(1, n_gz, greet_gz, 0)
    for step in (1, n_role - 1):
        pl.semaphore_signal(
            barrier, inc=1, device_id={"role": lax.rem(role + step, n_role)}, device_id_type=MESH
        )

    pairs = (
        (tr_hbm, tr_v),
        (ro_hbm, ro_v),
        (own_hbm, own_v),
        (p_hbm, p_v),
        (al_hbm, c0_v),
        (vn_hbm, c1_v),
        (ks_hbm, ks_v),
        (po_hbm, po_v),
        (lt_hbm, lt_v),
        (ai_hbm, ai_v),
    )
    loads = [pltpu.make_async_copy(a, b, load_sem.at[i]) for i, (a, b) in enumerate(pairs)]
    for load in loads:
        load.start()

    loads[0].wait()
    loads[1].wait()
    for b in range(n_gx):
        tp_v[b, CAP:4, :] = jnp.zeros((1, cols), jnp.float32)
        tp_v[b, 4 + CAP :, :] = jnp.zeros((1, cols), jnp.float32)
        tp_v[b, 0:CAP, :] = tr_v[b * CAP : (b + 1) * CAP, :]
        tp_v[b, 4 : 4 + CAP, :] = ro_v[b * CAP : (b + 1) * CAP, :].astype(jnp.float32)

    loads[2].wait()
    lane1 = lax.broadcasted_iota(jnp.int32, (1, 128), 1)
    sub4 = lax.broadcasted_iota(jnp.int32, (n_role, 128), 0)

    def role_lanes(start):
        return jnp.sum(
            jnp.where(sub4 == role, own_v[:, pl.ds(start, 128)], 0), axis=0, keepdims=True
        )

    pair = role_lanes(pl.multiple_of((gx // 2) * 128, 128))
    own = jnp.where(lax.rem(gx, 2) == 1, pltpu.roll(pair, 64, 1), pair)
    ii = lax.broadcasted_iota(jnp.int32, (128, 128), 0)
    jj = lax.broadcasted_iota(jnp.int32, (128, 128), 1)
    by_lane = jnp.broadcast_to(own, (128, 128))
    by_sub = jnp.transpose(by_lane)
    earlier = (by_lane == by_sub) & (ii < jj) & (ii < rows)
    rank_lane = jnp.sum(jnp.where(earlier, 1, 0), axis=0, keepdims=True)
    rank_sub = jnp.transpose(jnp.broadcast_to(rank_lane, (128, 128)))
    key = jnp.where((own >= 0) & (lane1 < rows), own * CAP + rank_lane + 1, 0)
    key = jnp.broadcast_to(key + pltpu.roll(key, 64, 1), (groups * CAP, 128))
    slot = lax.broadcasted_iota(jnp.int32, (groups * CAP, 128), 0) + 1
    wide = lax.broadcasted_iota(jnp.int32, (groups * CAP, 128), 1)
    pick = key == slot
    sel_v[:, 0:128] = jnp.where(pick, 1.0, 0.0).astype(jnp.bfloat16)
    sel_v[:, 128:256] = jnp.where(pick & (wide < rows), 1.0, 0.0).astype(jnp.bfloat16)
    at = jnp.where(by_sub >= 0, by_sub * 8 + rank_sub, -8)[:rows]
    for t in range(groups * 8 // 128):
        for f in range(2):
            hit = at + 4 * f == jj[:rows] + t * 128
            get_v[f * rows : (f + 1) * rows, t * 128 : (t + 1) * 128] = jnp.where(
                hit, 1.0, 0.0
            ).astype(jnp.bfloat16)
    act_v[...] = jnp.where(by_sub[:rows] >= 0, 1.0, 0.0)
    for t in range(n_gx // 2):
        hit = jnp.where(role_lanes(t * 128) == me, 1.0, 0.0)
        for side in range(2):
            part = jnp.where((lane1 < 64) == (side == 0), hit, 0.0)
            cnt_v[2 * t + side : 2 * t + side + 1, :] = jnp.broadcast_to(
                jnp.sum(part, axis=1, keepdims=True), (1, 128)
            )

    lane = lax.broadcasted_iota(jnp.int32, (CHUNK, 128), 1)

    def pack_y(k, d, r0, level, head, cond):
        at0 = level - 1
        edge = 0 if d == 0 else 127
        h = pltpu.roll(head, at0 + (128 - edge if edge else 0), 1)
        c = pltpu.roll(cond, at0 + levels + (128 - edge if edge else 0), 1)
        old = ys[k, d, pl.ds(r0, CHUNK), :]
        ys[k, d, pl.ds(r0, CHUNK), :] = jnp.where(
            lane == at0, h, jnp.where(lane == at0 + levels, c, old)
        )

    def put(k, level, r0, head, cond):
        hp[k, level, pl.ds(PAD + r0, CHUNK), :] = head
        kp[k, level, pl.ds(PAD + r0, CHUNK), :] = cond
        at0 = level - 1
        if r0 == 0:
            xs[k, 0, 0, pl.ds(at0, 1), :] = head[0:1]
            xs[k, 0, 1, pl.ds(at0, 1), :] = cond[0:1]
        if r0 + CHUNK == rows:
            xs[k, 1, 0, pl.ds(at0, 1), :] = head[CHUNK - 1 :]
            xs[k, 1, 1, pl.ds(at0, 1), :] = cond[CHUNK - 1 :]
        for d in range(2):
            pack_y(k, d, r0, level, head, cond)

    def remote(src, dst, k, slot, dst_slot, where):
        return pltpu.make_async_remote_copy(
            src_ref=src,
            dst_ref=dst,
            send_sem=h_send.at[k * 8 + slot],
            recv_sem=h_recv.at[k * 8 + dst_slot],
            device_id=where,
            device_id_type=MESH,
        )

    def faces_z(k):
        made = []
        for d in range(2):
            to = lax.rem(gz + (n_gz - 1 if d == 0 else 1), n_gz)
            for f, ref in enumerate((hp, kp)):
                src = ref.at[k, 1 if d == 0 else levels, pl.ds(PAD, rows), :]
                dst = ref.at[k, levels + 1 if d == 0 else 0, pl.ds(PAD, rows), :]
                made.append(remote(src, dst, k, 4 + 2 * f + d, 4 + 2 * f + 1 - d, {"gz": to}))
        return made

    def faces_xy(k):
        made = []
        for d in range(2):
            to = lax.rem(gx + (n_gx - 1 if d == 0 else 1), n_gx)
            made.append(remote(xs.at[k, d], xh.at[k, 1 - d], k, d, 1 - d, {"gx": to}))
        for d in range(2):
            to = lax.rem(role + (n_role - 1 if d == 0 else 1), n_role)
            made.append(remote(ys.at[k, d], yh.at[k, 1 - d], k, 2 + d, 2 + 1 - d, {"role": to}))
        return made

    mean_v[:, CAP * rows :, :] = jnp.zeros((layers, 256 - CAP * rows, 2 * cols), jnp.bfloat16)
    for load in loads[3:8]:
        load.wait()

    def start_layer(j, c):
        for r0 in range(0, rows, CHUNK):
            rs = pl.ds(r0, CHUNK)
            sum_s = None
            sum_h = None
            for i in range(LEVELS_PER_LAYER):
                z = j * LEVELS_PER_LAYER + i
                head = p_v[z, rs, :]
                vn = c1_v[z, rs, :]
                c0 = vn * jnp.log(c0_v[z, rs, :]) * LOG2E
                c1 = (0.5 * LOG2E) * vn
                m = 1.0 - 1.0 / vn
                ks = 0.5 * ks_v[z, rs, :]
                c0_v[z, rs, :] = c0
                c1_v[z, rs, :] = c1
                m_v[z, rs, :] = m
                ks_v[z, rs, :] = ks
                sat, cond = curves(head, c1, c0, m, ks)
                th_v[z, rs, :] = po_v[z, rs, :] * sat
                put(0, z + 1, r0, head, cond)
                sum_s = sat if sum_s is None else sum_s + sat
                sum_h = head if sum_h is None else sum_h + head
            mean_h = sum_h * 0.25
            lh_v[j, rs, :] = mean_h
            for f, mean in enumerate((mean_h, sum_s * 0.25)):
                for part, value in enumerate(split3(mean)):
                    mean_v[j, part * rows + r0 : part * rows + r0 + CHUNK, f * cols : (f + 1) * cols] = value
        return c

    started = []
    lax.fori_loop(0, 2, lambda i, c: start_layer(i * (layers - 1), c), 0)

    pl.semaphore_wait(barrier, (n_gx - 1) + (n_gz - 1) + 2)

    def tell_line(i, c):
        pl.semaphore_signal(
            line_sem, inc=1, device_id={"gz": lax.rem(gz + i, n_gz)}, device_id_type=MESH
        )
        return c

    lax.fori_loop(1, n_gz, tell_line, 0)

    def zt_copy(i):
        to = lax.rem(gx + i, n_gx)
        return pltpu.make_async_remote_copy(
            src_ref=tp_v.at[to],
            dst_ref=rt_v.at[gx, gz],
            send_sem=zt_send,
            recv_sem=zt_recv,
            device_id={"gx": to},
            device_id_type=MESH,
        )

    def zt_start(i, c):
        zt_copy(i).start()
        return c

    lax.fori_loop(1, n_gx, zt_start, 0)
    rt_v[gx, gz] = tp_v[gx]

    for copy in faces_z(0):
        copy.start()
        started.append(copy)
    lax.fori_loop(1, layers - 1, start_layer, 0)
    for copy in faces_xy(0):
        copy.start()
        started.append(copy)

    for j in range(layers):
        out = jnp.dot(sel_v[...], mean_v[j], preferred_element_type=jnp.float32)
        tx_v[pl.ds(j, groups * CAP, stride=tile), :] = out[:, :cols]
        tx_v[pl.ds(layers + j, groups * CAP, stride=tile), :] = out[:, cols:]
    rx_v[pl.ds(pl.multiple_of(me * per, 8), per), :] = tx_v[
        pl.ds(pl.multiple_of(me * per, 8), per), :
    ]
    pl.semaphore_wait(line_sem, n_gz - 1)

    def land_start(i, c):
        to_gx = lax.rem(gx + i // n_gz, n_gx)
        to_gz = lax.rem(gz + lax.rem(i, n_gz), n_gz)
        to = to_gx * n_gz + to_gz
        pltpu.make_async_remote_copy(
            src_ref=tx_v.at[pl.ds(pl.multiple_of(to * per, 8), per), :],
            dst_ref=rx_v.at[pl.ds(pl.multiple_of(me * per, 8), per), :],
            send_sem=land_send,
            recv_sem=land_recv,
            device_id={"gx": to_gx, "gz": to_gz},
            device_id_type=MESH,
        ).start()
        return c

    cut1 = groups // 4
    cut2 = groups // 2
    lax.fori_loop(1, cut1, land_start, 0)

    def drain(ref, count, sem):
        pltpu.make_async_copy(ref.at[pl.ds(0, count)], ref.at[pl.ds(0, count)], sem).wait()

    drain(tp_v, n_gx - 1, zt_recv)

    def xt_copy(i):
        return pltpu.make_async_remote_copy(
            src_ref=rt_v.at[:, gz],
            dst_ref=rt_v.at[:, gz],
            send_sem=xt_send,
            recv_sem=xt_recv,
            device_id={"gz": lax.rem(gz + i, n_gz)},
            device_id_type=MESH,
        )

    for i in range(1, n_gz):
        xt_copy(i).start()

    at_lo = role > 0
    at_hi = role < n_role - 1

    def wait_faces(k):
        for slot, ref in ((0, xh.at[k, 0]), (1, xh.at[k, 1]), (2, yh.at[k, 0]), (3, yh.at[k, 1])):
            pltpu.make_async_copy(ref, ref, h_recv.at[k * 8 + slot]).wait()
        for f, ref in enumerate((hp, kp)):
            for d in range(2):
                view = ref.at[k, 0 if d == 0 else levels + 1, pl.ds(PAD, rows), :]
                pltpu.make_async_copy(view, view, h_recv.at[k * 8 + 4 + 2 * f + d]).wait()

        @pl.when(gz == 0)
        def _():
            hp[k, 0, pl.ds(PAD, rows), :] = hp[k, 1, pl.ds(PAD, rows), :]
            kp[k, 0, pl.ds(PAD, rows), :] = -kp[k, 1, pl.ds(PAD, rows), :]

        @pl.when(gz == n_gz - 1)
        def _():
            hp[k, levels + 1, pl.ds(PAD, rows), :] = hp[k, levels, pl.ds(PAD, rows), :]
            kp[k, levels + 1, pl.ds(PAD, rows), :] = -kp[k, levels, pl.ds(PAD, rows), :]

    def put_rows(k, level):
        at0 = pl.ds(level - 1, 1)
        for d, row, edge, inside in ((0, PAD - 1, PAD, gx > 0), (1, PAD + rows, PAD + rows - 1, gx < n_gx - 1)):
            hp[k, level, row : row + 1, :] = jnp.where(
                inside, xh[k, d, 0, at0, :], hp[k, level, edge : edge + 1, :]
            )
            kp[k, level, row : row + 1, :] = jnp.where(
                inside, xh[k, d, 1, at0, :], -kp[k, level, edge : edge + 1, :]
            )

    def stencil(k, level, r0):
        def cut(ref, z, shift):
            return ref[k, z, pl.ds(PAD + r0 + shift, CHUNK), :]

        h, c = cut(hp, level, 0), cut(kp, level, 0)
        kf_up = c + cut(kp, level - 1, 0)
        kf_dn = c + cut(kp, level + 1, 0)
        kf_xm = c + cut(kp, level, -1)
        kf_xp = c + cut(kp, level, 1)
        at0 = level - 1
        side0 = yh[k, 0, pl.ds(r0, CHUNK), :]
        side1 = yh[k, 1, pl.ds(r0, CHUNK), :]
        first, last = lane == 0, lane == 127
        h_ym = jnp.where(
            first, jnp.where(at_lo, pltpu.roll(side0, 128 - at0, 1), h), pltpu.roll(h, 1, 1)
        )
        c_ym = jnp.where(
            first,
            jnp.where(at_lo, pltpu.roll(side0, 128 - levels - at0, 1), -c),
            pltpu.roll(c, 1, 1),
        )
        h_yp = jnp.where(
            last, jnp.where(at_hi, pltpu.roll(side1, 127 - at0, 1), h), pltpu.roll(h, 127, 1)
        )
        c_yp = jnp.where(
            last,
            jnp.where(at_hi, pltpu.roll(side1, 127 - levels - at0, 1), -c),
            pltpu.roll(c, 127, 1),
        )
        kf_ym = c + c_ym
        kf_yp = c + c_yp
        flux = kf_up * (h - cut(hp, level - 1, 0)) + kf_dn * (h - cut(hp, level + 1, 0))
        flux = flux + kf_xm * (h - cut(hp, level, -1)) + kf_xp * (h - cut(hp, level, 1))
        flux = flux + kf_ym * (h - h_ym) + kf_yp * (h - h_yp)
        diag = 1.0 + ((kf_up + kf_dn) + (kf_xm + kf_xp) + (kf_ym + kf_yp))
        return h, flux + (kf_dn - kf_up), diag

    wait_faces(0)

    def first_half(z, c):
        level = z + 1
        put_rows(0, level)
        for r0 in range(0, rows, CHUNK):
            _, resid, diag = stencil(0, level, r0)
            ra_v[z, pl.ds(r0, CHUNK), :] = resid
            da_v[z, pl.ds(r0, CHUNK), :] = OMEGAS[0] / diag
        return c

    lax.fori_loop(0, levels, first_half, 0)
    lax.fori_loop(cut1, cut2, land_start, 0)

    ref3 = rt_v.at[:, pl.ds(0, n_gz - 1)]
    pltpu.make_async_copy(ref3, ref3, xt_recv).wait()

    pieces = jnp.concatenate(split3(rt_v[...].reshape(groups * 8, cols)), axis=1)
    got = jnp.dot(get_v[...], pieces, preferred_element_type=jnp.float32)
    got = got[:, :cols] + got[:, cols : 2 * cols] + got[:, 2 * cols :]
    tq_v[...] = got[:rows]
    rq_v[...] = got[rows:] + (1.0 - act_v[...])

    def root_weight(depth, roots):
        return jnp.where(depth < roots, math.exp(-depth / 4.0), 0.0)

    for r0 in range(0, rows, CHUNK):
        rs = pl.ds(r0, CHUNK)
        roots = rq_v[rs, :]
        total = root_weight(0, roots)
        for depth in range(1, layers * n_gz):
            total = total + root_weight(depth, roots)
        scale = tq_v[rs, :]
        for j in range(layers):
            depth = (gz * layers + j).astype(jnp.float32)
            weight = jnp.where(
                depth < roots, jnp.exp(jnp.full((CHUNK, 128), -0.25, jnp.float32) * depth), 0.0
            )
            lh = lh_v[j, rs, :]
            stress = 1.0 / (1.0 + lh * lh * (1.0 / 2.25))
            sk_v[j, rs, :] = scale * (weight / total) * stress

    def curve_into(k, z, r0, head):
        rs = pl.ds(r0, CHUNK)
        sat, cond = curves(head, c1_v[z, rs, :], c0_v[z, rs, :], m_v[z, rs, :], ks_v[z, rs, :])
        put(k, z + 1, r0, head, cond)
        ra_v[z, rs, :] = (po_v[z, rs, :] * sat - th_v[z, rs, :]) + sk_v[
            z // LEVELS_PER_LAYER, rs, :
        ]

    def second_half(z, c):
        for r0 in range(0, rows, CHUNK):
            rs = pl.ds(r0, CHUNK)
            resid = ra_v[z, rs, :] + sk_v[z // LEVELS_PER_LAYER, rs, :]
            curve_into(1, z, r0, p_v[z, rs, :] - resid * da_v[z, rs, :])
        return c

    def sweep_level(k, z, c):
        level = z + 1
        put_rows(k, level)
        for r0 in range(0, rows, CHUNK):
            rs = pl.ds(r0, CHUNK)
            head, flux, diag = stencil(k, level, r0)
            head = head - (ra_v[z, rs, :] + flux) * (OMEGAS[k] / diag)
            if k + 1 < SWEEPS:
                curve_into(k + 1, z, r0, head)
            else:
                out_p[z, rs, :] = head
        return c

    def run(k, body):
        lax.fori_loop(0, 2, lambda i, c: body(i * (levels - 1), c), 0)
        for copy in faces_z(k + 1):
            copy.start()
            started.append(copy)
        lax.fori_loop(1, levels - 1, body, 0)
        for copy in faces_xy(k + 1):
            copy.start()
            started.append(copy)

    run(0, second_half)
    lax.fori_loop(cut2, groups, land_start, 0)
    for k in range(1, SWEEPS):
        wait_faces(k)
        if k + 1 < SWEEPS:
            run(k, functools.partial(sweep_level, k))
        else:
            lax.fori_loop(0, levels, functools.partial(sweep_level, k), 0)

    for load in loads[8:]:
        load.wait()
    all_but_me = rx_v.at[pl.ds(0, (groups - 1) * per), :]
    pltpu.make_async_copy(all_but_me, all_but_me, land_recv).wait()
    sub = min(8, n_gx)
    n_layers = layers * n_gz
    for half in range(n_gx // sub):
        for r in range(CAP):
            b0 = half * sub

            def slots(ref, at3, stride):
                return ref[pl.ds(at3, sub, stride=stride), :]

            tpot = slots(tr_v, b0 * CAP + r, CAP)
            air = slots(ai_v, b0 * CAP + r, CAP)
            roots = slots(ro_v, b0 * CAP + r, CAP).astype(jnp.float32)
            weights = [root_weight(d, roots) for d in range(n_layers)]
            total = weights[0]
            for weight in weights[1:]:
                total = total + weight
            temps, kappa, upt = [], [], []
            for d in range(n_layers):
                bz, j = d // layers, d % layers
                base = (b0 * n_gz + bz) * per + r * tile + j
                lh = slots(rx_v, base, n_gz * per)
                ls = slots(rx_v, base + layers, n_gz * per)
                stress = 1.0 / (1.0 + lh * lh * (1.0 / 2.25))
                upt.append(0.3 * (tpot * (weights[d] / total) * stress))
                kappa.append(0.25 + 0.9 * ls)
                temps.append(slots(lt_v, (b0 * CAP + r) * n_layers + d, CAP * n_layers))
            mids = [0.5 * (kappa[d] + kappa[d + 1]) for d in range(n_layers - 1)]
            old = temps
            for _ in range(HEAT_STEPS):
                fresh = []
                for d in range(n_layers):
                    move = (
                        kappa[0] * (air - temps[0])
                        if d == 0
                        else mids[d - 1] * (temps[d - 1] - temps[d])
                    )
                    if d < n_layers - 1:
                        move = move + mids[d] * (temps[d + 1] - temps[d])
                    fresh.append(temps[d] + 0.2 * move - upt[d])
                temps = fresh
            filled = cnt_v[b0 : b0 + sub, :] > r
            for d in range(n_layers):
                out_lt[pl.ds((b0 * CAP + r) * n_layers + d, sub, stride=CAP * n_layers), :] = (
                    jnp.where(filled, temps[d], old[d])
                )

    for copy in started:
        copy.wait_send()
    drain(tp_v, n_gx - 1, zt_send)
    pltpu.make_async_copy(ref3, ref3, xt_send).wait()
    pltpu.make_async_copy(all_but_me, all_but_me, land_send).wait()


def solution(mesh):
    n_role, n_gx, n_gz = (mesh.shape[a] for a in ("role", "gx", "gz"))

    def local(p, al, vn, ks, po, owner, land, transp, air, roots):
        levels, rows, cols = p.shape
        layers = levels // LEVELS_PER_LAYER
        n_layers = layers * n_gz
        groups = n_gx * n_gz
        slots = n_gx * CAP
        f32 = jnp.float32
        cell = pltpu.VMEM((levels, rows, cols), f32)
        padded = pltpu.VMEM((SWEEPS, levels + 2, rows + 2 * PAD, cols), f32)
        xface = pltpu.VMEM((SWEEPS, 2, 2, levels, cols), f32)
        yface = pltpu.VMEM((SWEEPS, 2, rows, cols), f32)
        line = pltpu.VMEM((slots, cols), f32)
        payload = pltpu.VMEM((groups * CAP * 2 * layers, cols), f32)
        dma = pltpu.SemaphoreType.DMA
        head, temps = pl.pallas_call(
            functools.partial(kernel, n_role, n_gx, n_gz),
            out_shape=(
                jax.ShapeDtypeStruct(p.shape, f32),
                jax.ShapeDtypeStruct((slots * n_layers, cols), f32),
            ),
            in_specs=[pl.BlockSpec(memory_space=pl.ANY)] * 10,
            out_specs=[pl.BlockSpec(memory_space=pltpu.VMEM)] * 2,
            scratch_shapes=[
                cell,
                cell,
                cell,
                cell,
                cell,
                cell,
                cell,
                cell,
                cell,
                padded,
                padded,
                xface,
                xface,
                yface,
                yface,
                pltpu.VMEM(owner.shape[::-1], jnp.int32),
                pltpu.VMEM((slots * n_layers, cols), f32),
                line,
                line,
                pltpu.VMEM((slots, cols), jnp.int32),
                pltpu.VMEM((groups * CAP, 256), jnp.bfloat16),
                pltpu.VMEM((2 * rows, groups * 8), jnp.bfloat16),
                pltpu.VMEM((rows, cols), f32),
                pltpu.VMEM((n_gx, cols), f32),
                pltpu.VMEM((n_gx, 8, cols), f32),
                pltpu.VMEM((n_gx, n_gz, 8, cols), f32),
                pltpu.VMEM((rows, cols), f32),
                pltpu.VMEM((rows, cols), f32),
                pltpu.VMEM((layers, rows, cols), f32),
                pltpu.VMEM((layers, rows, cols), f32),
                pltpu.VMEM((layers, 256, 2 * cols), jnp.bfloat16),
                payload,
                payload,
                dma((10,)),
                dma,
                dma,
                dma,
                dma,
                dma((SWEEPS * 8,)),
                dma((SWEEPS * 8,)),
                dma,
                dma,
                pltpu.SemaphoreType.REGULAR,
            ],
            compiler_params=pltpu.CompilerParams(
                collective_id=0, has_side_effects=True, vmem_limit_bytes=56 * 1024 * 1024
            ),
        )(
            p,
            al,
            vn,
            ks,
            po,
            owner.T,
            land.reshape(slots * n_layers, cols),
            transp.reshape(slots, cols),
            air.reshape(slots, cols),
            roots.reshape(slots, cols),
        )
        return head, temps.reshape(land.shape)

    grid = P("gz", "gx", "role")
    slot = P("role", ("gx", "gz"), None, None)
    return jax.shard_map(
        local,
        mesh=mesh,
        in_specs=(grid,) * 5 + (P(), P("role", ("gx", "gz"), None, None, None)) + (slot,) * 3,
        out_specs=(grid, P("role", ("gx", "gz"), None, None, None)),
        check_vma=False,
    )
```

time: 242 us -> 49.2 us (0.20)
  waiting for transfers between devices: 76.4 us -> 0 us
  starting transfers between devices: 71.3 us -> 0 us
  Pallas kernels: 0 us -> 45.7 us
  local copies, waits for them, and re-layouts: 48.1 us -> 2.68 us
  other arithmetic: 42.3 us -> 0 us
    ppermute x18 -> x0, waiting for transfers between devices: 67.6 us -> none  [the longest x9 45.4 us: with_halo(): lax.ppermute(tail, axis, [(i, (i + 1) % count) for i in range(ends)])]
    ppermute x18 -> x0, starting transfers between devices: 47 us -> none  [the longest x9 33.1 us: with_halo(): lax.ppermute(tail, axis, [(i, (i + 1) % count) for i in range(ends)])]
    pallas_call x0 -> x1, Pallas kernels: none -> 45.7 us  [local(): pl.pallas_call(functools.partial(kernel, n_role, n_gx, n_gz), out_shape=(...]
    all_to_all x2 -> x0, starting transfers between devices: 24.4 us -> none  [the longest x1 13.3 us: local(): lax.all_to_all(outgoing.reshape((groups, CAP) + payload.shape[1:]), ('gx'...]
    slice x21 -> x0, local copies, waits for them, and re-layouts: 19.9 us -> none  [the longest x1 8.66 us: layer_mean(): first = lax.index_in_dim(parts, 0, axis + 1, keepdims=False)]
    another operation x7 -> x0, other arithmetic: 16.1 us -> none  [the longest x6 14.2 us: local(): jnp.stack([head, cond])]
    all_to_all x2 -> x0, waiting for transfers between devices: 8.83 us -> none  [the longest x1 8.82 us: local(): lax.all_to_all(returning.reshape(groups, CAP, local_layers, columns), ('g...]
    scatter x1 -> x0, local copies, waits for them, and re-layouts: 8.38 us -> none  [local(): outgoing = jnp.zeros((groups * CAP,) + payload.shape[1:], jnp.float32).at...]
  transfers between devices with their start and end apart: 20 -> 0, of which waited for: 11 -> 0; matrix products, arithmetic and copies ran while one was open for 13% -> 0% of each run, Pallas kernels for 0% -> 0%
where the time goes in v1:
time: 49.2 us; the launch traced here: 49.1 us
  Pallas kernels  45.7 us (93%)
  local copies, waits for them, and re-layouts  2.68 us (5%)
  between operations  0.65 us (1%)
    pallas_call x1, Pallas kernels, local(): pl.pallas_call(functools.partial(kernel, n_role, n_gx, n_gz), out_shape=(...  45.7 us
    unnamed x4, local copies, waits for them, and re-layouts  2.68 us

profile of v1, /device:TPU:1, one launch (start us, length us, event | category | flops | bytes accessed | tf_op | source)
XLA Modules:
  0.0 49.1 jit_solution(13438588591392758876)
XLA Ops:
  0.6 45.7 %shard_map.113 = (f32[16,64,128]{2,1,0:T(8,128)}, f32[768,128]{1,0:T(8,128)}) custom-call(f32[16,64,128]{2,1,0:T(8,128)} %p_hbm.1, f32[16,64,128]{2,1,0:T(8,128)} %al_hbm.1, f32[16,64,128]{2,1,0:T(8,128)} %vn_hbm.1, f32[16,64,128]{2,1,0:T(8,128)} %ks_hbm.1, f32[16,64,128]{2,1,0:T(8,128)} %po_hbm.1, s32[4,1024]{1,0:T(4,128)} %bitcast.11, f32[768,128]{1,0:T(8,128)} %bitcast.6, ...), custom_call_target="tpu_custom_call" | custom-call | tf_op jit(solution)/shard_map/pallas_call | solution.py:598
  46.4 0.0 copy-start
  46.4 1.9 %copy.14 = f32[16,64,128]{2,1,0:T(8,128)} copy(f32[16,64,128]{2,1,0:T(8,128)} %get-tuple-element.8) | data formatting | bytes 1048576
  48.3 0.0 copy-done
  48.3 0.7 %copy.15 = f32[1,1,48,16,128]{4,3,2,1,0:T(8,128)} copy(f32[1,1,48,16,128]{4,3,2,1,0:T(8,128)S(1)} %bitcast.7) | data formatting | bytes 786432
Async XLA Ops:
  46.4 1.9 %copy-start = (f32[768,128]{1,0:T(8,128)S(1)}, f32[768,128]{1,0:T(8,128)}, u32[]{:S(2)}) copy-start(f32[768,128]{1,0:T(8,128)} %get-tuple-element.5) | copy-start | bytes 1179652

commit v2 on v1

--- a/solution.py
+++ b/solution.py
@@ -14,6 +14,7 @@
 HEAT_STEPS = 4
 LOG2E = 1.0 / math.log(2.0)
 CHUNK = 32
+PARTS = 2
 PAD = 8
 MESH = pl.DeviceIdType.MESH
 OMEGAS = [
@@ -21,8 +22,8 @@
 ]
 
 
-def curves(head, c1, c0, m, ks):
-    lx = c1 * jnp.log(head * head + 0.01) + c0
+def curves(head, la, vn, m, ks):
+    lx = vn * (la + (0.5 * LOG2E) * jnp.log(head * head + 0.01))
     soft = jnp.log(1.0 + jnp.exp2(lx)) * LOG2E
     root = jnp.exp2(-0.5 * (m * soft))
     gap = 1.0 - jnp.exp2(m * (lx - soft))
@@ -52,17 +53,20 @@
     ro_hbm,
     out_p,
     out_lt,
-    p_v,
-    c0_v,
-    c1_v,
+    la_v,
+    vn_v,
     ks_v,
     po_v,
     m_v,
     th_v,
     ra_v,
     da_v,
-    hp,
-    kp,
+    hp0,
+    hp1,
+    hp2,
+    kp0,
+    kp1,
+    kp2,
     xs,
     xh,
     ys,
@@ -105,6 +109,9 @@
     gx = lax.axis_index("gx")
     gz = lax.axis_index("gz")
     me = gx * n_gz + gz
+    hp = (hp0, hp1, hp2)
+    kp = (kp0, kp1, kp2)
+    half = levels // PARTS
 
     barrier = pltpu.get_barrier_semaphore()
 
@@ -131,9 +138,9 @@
         (tr_hbm, tr_v),
         (ro_hbm, ro_v),
         (own_hbm, own_v),
-        (p_hbm, p_v),
-        (al_hbm, c0_v),
-        (vn_hbm, c1_v),
+        (p_hbm, hp0.at[pl.ds(1, levels), pl.ds(PAD, rows), :]),
+        (al_hbm, la_v),
+        (vn_hbm, vn_v),
         (ks_hbm, ks_v),
         (po_hbm, po_v),
         (lt_hbm, lt_v),
@@ -177,11 +184,12 @@
     sel_v[:, 0:128] = jnp.where(pick, 1.0, 0.0).astype(jnp.bfloat16)
     sel_v[:, 128:256] = jnp.where(pick & (wide < rows), 1.0, 0.0).astype(jnp.bfloat16)
     at = jnp.where(by_sub >= 0, by_sub * 8 + rank_sub, -8)[:rows]
-    for t in range(groups * 8 // 128):
+    width = min(128, groups * 8)
+    for t in range(groups * 8 // width):
         for f in range(2):
-            hit = at + 4 * f == jj[:rows] + t * 128
-            get_v[f * rows : (f + 1) * rows, t * 128 : (t + 1) * 128] = jnp.where(
-                hit, 1.0, 0.0
+            hit = at + 4 * f == jj[:rows] + t * width
+            get_v[f * rows : (f + 1) * rows, t * width : (t + 1) * width] = jnp.where(
+                hit[:, :width], 1.0, 0.0
             ).astype(jnp.bfloat16)
     act_v[...] = jnp.where(by_sub[:rows] >= 0, 1.0, 0.0)
     for t in range(n_gx // 2):
@@ -192,96 +200,134 @@
                 jnp.sum(part, axis=1, keepdims=True), (1, 128)
             )
 
-    lane = lax.broadcasted_iota(jnp.int32, (CHUNK, 128), 1)
-
-    def pack_y(k, d, r0, level, head, cond):
-        at0 = level - 1
-        edge = 0 if d == 0 else 127
-        h = pltpu.roll(head, at0 + (128 - edge if edge else 0), 1)
-        c = pltpu.roll(cond, at0 + levels + (128 - edge if edge else 0), 1)
-        old = ys[k, d, pl.ds(r0, CHUNK), :]
-        ys[k, d, pl.ds(r0, CHUNK), :] = jnp.where(
-            lane == at0, h, jnp.where(lane == at0 + levels, c, old)
-        )
-
-    def put(k, level, r0, head, cond):
-        hp[k, level, pl.ds(PAD + r0, CHUNK), :] = head
-        kp[k, level, pl.ds(PAD + r0, CHUNK), :] = cond
-        at0 = level - 1
+    lane = lax.broadcasted_iota(jnp.int32, (8, 128), 1)
+    wide_lane = lax.broadcasted_iota(jnp.int32, (CHUNK, 128), 1)
+
+    def pack_y(k, d, part, r0, at0, head, cond):
+        face = ys[k, d, part]
+        for g in range(r0 // 8, (r0 + CHUNK) // 8):
+            for f, ref in enumerate((head, cond)):
+                to = g * 16 + f * half + at0
+                shift = to if d == 0 else jnp.bitwise_and(to + 1, 127)
+                face = jnp.where(
+                    lane == to, pltpu.roll(ref[g * 8 - r0 : g * 8 - r0 + 8], shift, 1), face
+                )
+        ys[k, d, part] = face
+
+    def take_y(k, d, part, r0, at0, f):
+        face = yh[k, d, part]
+        end = 128 if d == 0 else 127
+        return jnp.concatenate(
+            [
+                pltpu.roll(face, end - g * 16 - f * half - at0, 1)
+                for g in range(r0 // 8, (r0 + CHUNK) // 8)
+            ],
+            axis=0,
+        )
+
+    def put(k, part, z, r0, head, cond, keep_head=True):
+        if keep_head:
+            hp[k][z + 1, pl.ds(PAD + r0, CHUNK), :] = head
+        kp[k][z + 1, pl.ds(PAD + r0, CHUNK), :] = cond
+        at0 = z - part * half
         if r0 == 0:
-            xs[k, 0, 0, pl.ds(at0, 1), :] = head[0:1]
-            xs[k, 0, 1, pl.ds(at0, 1), :] = cond[0:1]
+            xs[k, 0, part, 0, pl.ds(at0, 1), :] = head[0:1]
+            xs[k, 0, part, 1, pl.ds(at0, 1), :] = cond[0:1]
         if r0 + CHUNK == rows:
-            xs[k, 1, 0, pl.ds(at0, 1), :] = head[CHUNK - 1 :]
-            xs[k, 1, 1, pl.ds(at0, 1), :] = cond[CHUNK - 1 :]
+            xs[k, 1, part, 0, pl.ds(at0, 1), :] = head[CHUNK - 1 :]
+            xs[k, 1, part, 1, pl.ds(at0, 1), :] = cond[CHUNK - 1 :]
         for d in range(2):
-            pack_y(k, d, r0, level, head, cond)
+            pack_y(k, d, part, r0, at0, head, cond)
 
     def remote(src, dst, k, slot, dst_slot, where):
         return pltpu.make_async_remote_copy(
             src_ref=src,
             dst_ref=dst,
-            send_sem=h_send.at[k * 8 + slot],
-            recv_sem=h_recv.at[k * 8 + dst_slot],
+            send_sem=h_send.at[k * 12 + slot],
+            recv_sem=h_recv.at[k * 12 + dst_slot],
             device_id=where,
             device_id_type=MESH,
         )
 
-    def faces_z(k):
+    started = []
+
+    def send(copies):
+        for copy in copies:
+            copy.start()
+        started.extend(copies)
+
+    def face_z(k, d):
+        to = lax.rem(gz + (n_gz - 1 if d == 0 else 1), n_gz)
         made = []
-        for d in range(2):
-            to = lax.rem(gz + (n_gz - 1 if d == 0 else 1), n_gz)
-            for f, ref in enumerate((hp, kp)):
-                src = ref.at[k, 1 if d == 0 else levels, pl.ds(PAD, rows), :]
-                dst = ref.at[k, levels + 1 if d == 0 else 0, pl.ds(PAD, rows), :]
-                made.append(remote(src, dst, k, 4 + 2 * f + d, 4 + 2 * f + 1 - d, {"gz": to}))
+        for f, ref in enumerate((hp[k], kp[k])):
+            src = ref.at[1 if d == 0 else levels, pl.ds(PAD, rows), :]
+            dst = ref.at[levels + 1 if d == 0 else 0, pl.ds(PAD, rows), :]
+            made.append(remote(src, dst, k, 8 + 2 * f + d, 8 + 2 * f + 1 - d, {"gz": to}))
         return made
 
-    def faces_xy(k):
+    def faces_xy(k, part):
         made = []
         for d in range(2):
             to = lax.rem(gx + (n_gx - 1 if d == 0 else 1), n_gx)
-            made.append(remote(xs.at[k, d], xh.at[k, 1 - d], k, d, 1 - d, {"gx": to}))
+            made.append(
+                remote(
+                    xs.at[k, d, part],
+                    xh.at[k, 1 - d, part],
+                    k,
+                    2 * part + d,
+                    2 * part + 1 - d,
+                    {"gx": to},
+                )
+            )
         for d in range(2):
             to = lax.rem(role + (n_role - 1 if d == 0 else 1), n_role)
-            made.append(remote(ys.at[k, d], yh.at[k, 1 - d], k, 2 + d, 2 + 1 - d, {"role": to}))
+            made.append(
+                remote(
+                    ys.at[k, d, part],
+                    yh.at[k, 1 - d, part],
+                    k,
+                    4 + 2 * part + d,
+                    4 + 2 * part + 1 - d,
+                    {"role": to},
+                )
+            )
         return made
 
     mean_v[:, CAP * rows :, :] = jnp.zeros((layers, 256 - CAP * rows, 2 * cols), jnp.bfloat16)
     for load in loads[3:8]:
         load.wait()
 
-    def start_layer(j, c):
+    def start_layer(part, i, c):
+        j = part * (layers // PARTS) + (layers // PARTS - 1 - i)
         for r0 in range(0, rows, CHUNK):
             rs = pl.ds(r0, CHUNK)
             sum_s = None
             sum_h = None
             for i in range(LEVELS_PER_LAYER):
                 z = j * LEVELS_PER_LAYER + i
-                head = p_v[z, rs, :]
-                vn = c1_v[z, rs, :]
-                c0 = vn * jnp.log(c0_v[z, rs, :]) * LOG2E
-                c1 = (0.5 * LOG2E) * vn
+                head = hp[0][z + 1, pl.ds(PAD + r0, CHUNK), :]
+                vn = vn_v[z, rs, :]
+                la = jnp.log(la_v[z, rs, :]) * LOG2E
                 m = 1.0 - 1.0 / vn
-                ks = 0.5 * ks_v[z, rs, :]
-                c0_v[z, rs, :] = c0
-                c1_v[z, rs, :] = c1
+                la_v[z, rs, :] = la
                 m_v[z, rs, :] = m
-                ks_v[z, rs, :] = ks
-                sat, cond = curves(head, c1, c0, m, ks)
+                sat, cond = curves(head, la, vn, m, ks_v[z, rs, :])
                 th_v[z, rs, :] = po_v[z, rs, :] * sat
-                put(0, z + 1, r0, head, cond)
+                put(0, part, z, r0, head, cond, keep_head=False)
                 sum_s = sat if sum_s is None else sum_s + sat
                 sum_h = head if sum_h is None else sum_h + head
             mean_h = sum_h * 0.25
             lh_v[j, rs, :] = mean_h
             for f, mean in enumerate((mean_h, sum_s * 0.25)):
-                for part, value in enumerate(split3(mean)):
-                    mean_v[j, part * rows + r0 : part * rows + r0 + CHUNK, f * cols : (f + 1) * cols] = value
-        return c
-
-    started = []
-    lax.fori_loop(0, 2, lambda i, c: start_layer(i * (layers - 1), c), 0)
+                for piece, value in enumerate(split3(mean)):
+                    mean_v[
+                        j,
+                        piece * rows + r0 : piece * rows + r0 + CHUNK,
+                        f * cols : (f + 1) * cols,
+                    ] = value
+        return c
+
+    lax.fori_loop(0, layers // PARTS, functools.partial(start_layer, 0), 0)
 
     pl.semaphore_wait(barrier, (n_gx - 1) + (n_gz - 1) + 2)
 
@@ -311,13 +357,9 @@
     lax.fori_loop(1, n_gx, zt_start, 0)
     rt_v[gx, gz] = tp_v[gx]
 
-    for copy in faces_z(0):
-        copy.start()
-        started.append(copy)
-    lax.fori_loop(1, layers - 1, start_layer, 0)
-    for copy in faces_xy(0):
-        copy.start()
-        started.append(copy)
+    send(face_z(0, 0) + faces_xy(0, 0))
+    lax.fori_loop(0, layers // PARTS, functools.partial(start_layer, 1), 0)
+    send(face_z(0, 1) + faces_xy(0, 1))
 
     for j in range(layers):
         out = jnp.dot(sel_v[...], mean_v[j], preferred_element_type=jnp.float32)
@@ -364,86 +406,74 @@
     for i in range(1, n_gz):
         xt_copy(i).start()
 
-    at_lo = role > 0
-    at_hi = role < n_role - 1
-
-    def wait_faces(k):
-        for slot, ref in ((0, xh.at[k, 0]), (1, xh.at[k, 1]), (2, yh.at[k, 0]), (3, yh.at[k, 1])):
-            pltpu.make_async_copy(ref, ref, h_recv.at[k * 8 + slot]).wait()
-        for f, ref in enumerate((hp, kp)):
-            for d in range(2):
-                view = ref.at[k, 0 if d == 0 else levels + 1, pl.ds(PAD, rows), :]
-                pltpu.make_async_copy(view, view, h_recv.at[k * 8 + 4 + 2 * f + d]).wait()
-
-        @pl.when(gz == 0)
+    sign = jnp.where(jnp.bitwise_and(lane, 15) < half, 1.0, -1.0)
+
+    def wait_part(k, part):
+        views = [(2 * part + d, xh.at[k, d, part]) for d in range(2)]
+        views += [(4 + 2 * part + d, yh.at[k, d, part]) for d in range(2)]
+        plane, edge = (0, 1) if part == 0 else (levels + 1, levels)
+        for f, ref in enumerate((hp[k], kp[k])):
+            views.append((8 + 2 * f + part, ref.at[plane, pl.ds(PAD, rows), :]))
+        for slot, view in views:
+            pltpu.make_async_copy(view, view, h_recv.at[k * 12 + slot]).wait()
+
+        @pl.when(gz == (0 if part == 0 else n_gz - 1))
         def _():
-            hp[k, 0, pl.ds(PAD, rows), :] = hp[k, 1, pl.ds(PAD, rows), :]
-            kp[k, 0, pl.ds(PAD, rows), :] = -kp[k, 1, pl.ds(PAD, rows), :]
-
-        @pl.when(gz == n_gz - 1)
-        def _():
-            hp[k, levels + 1, pl.ds(PAD, rows), :] = hp[k, levels, pl.ds(PAD, rows), :]
-            kp[k, levels + 1, pl.ds(PAD, rows), :] = -kp[k, levels, pl.ds(PAD, rows), :]
-
-    def put_rows(k, level):
-        at0 = pl.ds(level - 1, 1)
-        for d, row, edge, inside in ((0, PAD - 1, PAD, gx > 0), (1, PAD + rows, PAD + rows - 1, gx < n_gx - 1)):
-            hp[k, level, row : row + 1, :] = jnp.where(
-                inside, xh[k, d, 0, at0, :], hp[k, level, edge : edge + 1, :]
-            )
-            kp[k, level, row : row + 1, :] = jnp.where(
-                inside, xh[k, d, 1, at0, :], -kp[k, level, edge : edge + 1, :]
-            )
-
-    def stencil(k, level, r0):
-        def cut(ref, z, shift):
-            return ref[k, z, pl.ds(PAD + r0 + shift, CHUNK), :]
-
-        h, c = cut(hp, level, 0), cut(kp, level, 0)
-        kf_up = c + cut(kp, level - 1, 0)
-        kf_dn = c + cut(kp, level + 1, 0)
-        kf_xm = c + cut(kp, level, -1)
-        kf_xp = c + cut(kp, level, 1)
-        at0 = level - 1
-        side0 = yh[k, 0, pl.ds(r0, CHUNK), :]
-        side1 = yh[k, 1, pl.ds(r0, CHUNK), :]
-        first, last = lane == 0, lane == 127
-        h_ym = jnp.where(
-            first, jnp.where(at_lo, pltpu.roll(side0, 128 - at0, 1), h), pltpu.roll(h, 1, 1)
-        )
-        c_ym = jnp.where(
-            first,
-            jnp.where(at_lo, pltpu.roll(side0, 128 - levels - at0, 1), -c),
-            pltpu.roll(c, 1, 1),
-        )
-        h_yp = jnp.where(
-            last, jnp.where(at_hi, pltpu.roll(side1, 127 - at0, 1), h), pltpu.roll(h, 127, 1)
-        )
-        c_yp = jnp.where(
-            last,
-            jnp.where(at_hi, pltpu.roll(side1, 127 - levels - at0, 1), -c),
-            pltpu.roll(c, 127, 1),
-        )
+            hp[k][plane, pl.ds(PAD, rows), :] = hp[k][edge, pl.ds(PAD, rows), :]
+            kp[k][plane, pl.ds(PAD, rows), :] = -kp[k][edge, pl.ds(PAD, rows), :]
+
+        for d in range(2):
+
+            @pl.when(role == (0 if d == 0 else n_role - 1))
+            def _():
+                yh[k, d, part] = ys[k, d, part] * sign
+
+            @pl.when(gx == (0 if d == 0 else n_gx - 1))
+            def _():
+                xh[k, d, part, 0] = xs[k, d, part, 0]
+                xh[k, d, part, 1] = -xs[k, d, part, 1]
+
+        for d, row in ((0, PAD - 1), (1, PAD + rows)):
+            for f, ref in enumerate((hp[k], kp[k])):
+                for i in range(half):
+                    z = part * half + i
+                    ref[z + 1, row : row + 1, :] = xh[k, d, part, f, i : i + 1, :]
+
+    def stencil(k, part, z, r0):
+        def cut(ref, plane, shift):
+            return ref[k][plane, pl.ds(PAD + r0 + shift, CHUNK), :]
+
+        at0 = z - part * half
+        h, c = cut(hp, z + 1, 0), cut(kp, z + 1, 0)
+        first, last = wide_lane == 0, wide_lane == 127
+        c_ym = jnp.where(first, take_y(k, 0, part, r0, at0, 1), pltpu.roll(c, 1, 1))
+        c_yp = jnp.where(last, take_y(k, 1, part, r0, at0, 1), pltpu.roll(c, 127, 1))
+        h_ym = jnp.where(first, take_y(k, 0, part, r0, at0, 0), pltpu.roll(h, 1, 1))
+        h_yp = jnp.where(last, take_y(k, 1, part, r0, at0, 0), pltpu.roll(h, 127, 1))
+        c_up, c_dn = cut(kp, z, 0), cut(kp, z + 2, 0)
+        kf_up = c + c_up
+        kf_dn = c + c_dn
+        kf_xm = c + cut(kp, z + 1, -1)
+        kf_xp = c + cut(kp, z + 1, 1)
         kf_ym = c + c_ym
         kf_yp = c + c_yp
-        flux = kf_up * (h - cut(hp, level - 1, 0)) + kf_dn * (h - cut(hp, level + 1, 0))
-        flux = flux + kf_xm * (h - cut(hp, level, -1)) + kf_xp * (h - cut(hp, level, 1))
+        flux = kf_up * (h - cut(hp, z, 0)) + kf_dn * (h - cut(hp, z + 2, 0))
+        flux = flux + kf_xm * (h - cut(hp, z + 1, -1)) + kf_xp * (h - cut(hp, z + 1, 1))
         flux = flux + kf_ym * (h - h_ym) + kf_yp * (h - h_yp)
-        diag = 1.0 + ((kf_up + kf_dn) + (kf_xm + kf_xp) + (kf_ym + kf_yp))
-        return h, flux + (kf_dn - kf_up), diag
-
-    wait_faces(0)
-
-    def first_half(z, c):
-        level = z + 1
-        put_rows(0, level)
+        diag = 2.0 + ((kf_up + kf_dn) + (kf_xm + kf_xp) + (kf_ym + kf_yp))
+        return h, flux + (c_dn - c_up), diag
+
+    def first_half(part, i, c):
+        z = part * half + (half - 1 - i)
         for r0 in range(0, rows, CHUNK):
-            _, resid, diag = stencil(0, level, r0)
+            _, resid, diag = stencil(0, part, z, r0)
             ra_v[z, pl.ds(r0, CHUNK), :] = resid
             da_v[z, pl.ds(r0, CHUNK), :] = OMEGAS[0] / diag
         return c
 
-    lax.fori_loop(0, levels, first_half, 0)
+    for part in range(PARTS):
+        wait_part(0, part)
+        lax.fori_loop(0, half, functools.partial(first_half, part), 0)
     lax.fori_loop(cut1, cut2, land_start, 0)
 
     ref3 = rt_v.at[:, pl.ds(0, n_gz - 1)]
@@ -472,54 +502,46 @@
             )
             lh = lh_v[j, rs, :]
             stress = 1.0 / (1.0 + lh * lh * (1.0 / 2.25))
-            sk_v[j, rs, :] = scale * (weight / total) * stress
-
-    def curve_into(k, z, r0, head):
+            sk_v[j, rs, :] = 2.0 * (scale * (weight / total) * stress)
+
+    def curve_into(k, part, z, r0, head):
         rs = pl.ds(r0, CHUNK)
-        sat, cond = curves(head, c1_v[z, rs, :], c0_v[z, rs, :], m_v[z, rs, :], ks_v[z, rs, :])
-        put(k, z + 1, r0, head, cond)
-        ra_v[z, rs, :] = (po_v[z, rs, :] * sat - th_v[z, rs, :]) + sk_v[
-            z // LEVELS_PER_LAYER, rs, :
-        ]
-
-    def second_half(z, c):
+        sat, cond = curves(head, la_v[z, rs, :], vn_v[z, rs, :], m_v[z, rs, :], ks_v[z, rs, :])
+        put(k, part, z, r0, head, cond)
+        gain = po_v[z, rs, :] * sat - th_v[z, rs, :]
+        ra_v[z, rs, :] = (gain + gain) + sk_v[z // LEVELS_PER_LAYER, rs, :]
+
+    def second_half(part, i, c):
+        z = part * half + (half - 1 - i)
         for r0 in range(0, rows, CHUNK):
             rs = pl.ds(r0, CHUNK)
             resid = ra_v[z, rs, :] + sk_v[z // LEVELS_PER_LAYER, rs, :]
-            curve_into(1, z, r0, p_v[z, rs, :] - resid * da_v[z, rs, :])
-        return c
-
-    def sweep_level(k, z, c):
-        level = z + 1
-        put_rows(k, level)
+            head = hp[0][z + 1, pl.ds(PAD + r0, CHUNK), :]
+            curve_into(1, part, z, r0, head - resid * da_v[z, rs, :])
+        return c
+
+    def sweep_level(k, part, i, c):
+        z = part * half + (half - 1 - i)
         for r0 in range(0, rows, CHUNK):
             rs = pl.ds(r0, CHUNK)
-            head, flux, diag = stencil(k, level, r0)
+            head, flux, diag = stencil(k, part, z, r0)
             head = head - (ra_v[z, rs, :] + flux) * (OMEGAS[k] / diag)
             if k + 1 < SWEEPS:
-                curve_into(k + 1, z, r0, head)
+                curve_into(k + 1, part, z, r0, head)
             else:
                 out_p[z, rs, :] = head
         return c
 
-    def run(k, body):
-        lax.fori_loop(0, 2, lambda i, c: body(i * (levels - 1), c), 0)
-        for copy in faces_z(k + 1):
-            copy.start()
-            started.append(copy)
-        lax.fori_loop(1, levels - 1, body, 0)
-        for copy in faces_xy(k + 1):
-            copy.start()
-            started.append(copy)
-
-    run(0, second_half)
+    for part in range(PARTS):
+        lax.fori_loop(0, half, functools.partial(second_half, part), 0)
+        send(face_z(1, part) + faces_xy(1, part))
     lax.fori_loop(cut2, groups, land_start, 0)
     for k in range(1, SWEEPS):
-        wait_faces(k)
-        if k + 1 < SWEEPS:
-            run(k, functools.partial(sweep_level, k))
-        else:
-            lax.fori_loop(0, levels, functools.partial(sweep_level, k), 0)
+        for part in range(PARTS):
+            wait_part(k, part)
+            lax.fori_loop(0, half, functools.partial(sweep_level, k, part), 0)
+            if k + 1 < SWEEPS:
+                send(face_z(k + 1, part) + faces_xy(k + 1, part))
 
     for load in loads[8:]:
         load.wait()
@@ -527,9 +549,9 @@
     pltpu.make_async_copy(all_but_me, all_but_me, land_recv).wait()
     sub = min(8, n_gx)
     n_layers = layers * n_gz
-    for half in range(n_gx // sub):
+    for block in range(n_gx // sub):
         for r in range(CAP):
-            b0 = half * sub
+            b0 = block * sub
 
             def slots(ref, at3, stride):
                 return ref[pl.ds(at3, sub, stride=stride), :]
@@ -589,9 +611,9 @@
         slots = n_gx * CAP
         f32 = jnp.float32
         cell = pltpu.VMEM((levels, rows, cols), f32)
-        padded = pltpu.VMEM((SWEEPS, levels + 2, rows + 2 * PAD, cols), f32)
-        xface = pltpu.VMEM((SWEEPS, 2, 2, levels, cols), f32)
-        yface = pltpu.VMEM((SWEEPS, 2, rows, cols), f32)
+        padded = pltpu.VMEM((levels + 2, rows + 2 * PAD, cols), f32)
+        xface = pltpu.VMEM((SWEEPS, 2, PARTS, 2, levels // PARTS, cols), f32)
+        yface = pltpu.VMEM((SWEEPS, 2, PARTS, 8, cols), f32)
         line = pltpu.VMEM((slots, cols), f32)
         payload = pltpu.VMEM((groups * CAP * 2 * layers, cols), f32)
         dma = pltpu.SemaphoreType.DMA
@@ -612,7 +634,10 @@
                 cell,
                 cell,
                 cell,
-                cell,
+                padded,
+                padded,
+                padded,
+                padded,
                 padded,
                 padded,
                 xface,
@@ -642,8 +667,8 @@
                 dma,
                 dma,
                 dma,
-                dma((SWEEPS * 8,)),
-                dma((SWEEPS * 8,)),
+                dma((SWEEPS * 12,)),
+                dma((SWEEPS * 12,)),
                 dma,
                 dma,
                 pltpu.SemaphoreType.REGULAR,

time: 49.2 us -> 49.4 us (level)
  no operation moved by 1% of the time
where the time goes in v2:
time: 49.4 us; the launch traced here: 49.2 us
  Pallas kernels  45.9 us (93%)
  local copies, waits for them, and re-layouts  2.68 us (5%)
  between operations  0.65 us (1%)
    pallas_call x1, Pallas kernels, local(): pl.pallas_call(functools.partial(kernel, n_role, n_gx, n_gz), out_shape=(...  45.9 us
    unnamed x4, local copies, waits for them, and re-layouts  2.68 us

profile of v2, /device:TPU:1, one launch (start us, length us, event | category | flops | bytes accessed | tf_op | source)
XLA Modules:
  0.0 49.2 jit_solution(6816084147571660579)
XLA Ops:
  0.6 45.9 %shard_map.113 = (f32[16,64,128]{2,1,0:T(8,128)}, f32[768,128]{1,0:T(8,128)}) custom-call(f32[16,64,128]{2,1,0:T(8,128)} %p_hbm.1, f32[16,64,128]{2,1,0:T(8,128)} %al_hbm.1, f32[16,64,128]{2,1,0:T(8,128)} %vn_hbm.1, f32[16,64,128]{2,1,0:T(8,128)} %ks_hbm.1, f32[16,64,128]{2,1,0:T(8,128)} %po_hbm.1, s32[4,1024]{1,0:T(4,128)} %bitcast.11, f32[768,128]{1,0:T(8,128)} %bitcast.6, ...), custom_call_target="tpu_custom_call" | custom-call | tf_op jit(solution)/shard_map/pallas_call | solution.py:620
  46.6 0.0 copy-start
  46.6 1.9 %copy.14 = f32[16,64,128]{2,1,0:T(8,128)} copy(f32[16,64,128]{2,1,0:T(8,128)} %get-tuple-element.8) | data formatting | bytes 1048576
  48.5 0.0 copy-done
  48.5 0.7 %copy.15 = f32[1,1,48,16,128]{4,3,2,1,0:T(8,128)} copy(f32[1,1,48,16,128]{4,3,2,1,0:T(8,128)S(1)} %bitcast.7) | data formatting | bytes 786432
Async XLA Ops:
  46.6 1.9 %copy-start = (f32[768,128]{1,0:T(8,128)S(1)}, f32[768,128]{1,0:T(8,128)}, u32[]{:S(2)}) copy-start(f32[768,128]{1,0:T(8,128)} %get-tuple-element.5) | copy-start | bytes 1179652

commit v3 on v2

--- a/solution.py
+++ b/solution.py
@@ -15,6 +15,7 @@
 LOG2E = 1.0 / math.log(2.0)
 CHUNK = 32
 PARTS = 2
+PACE = (48, 0)
 PAD = 8
 MESH = pl.DeviceIdType.MESH
 OMEGAS = [
@@ -200,6 +201,19 @@
                 jnp.sum(part, axis=1, keepdims=True), (1, 128)
             )
 
+    segments = (
+        ((0, 2, lambda i: i * (levels - 1)), (2, half, lambda i: i - 1)),
+        ((0, half, lambda i: half - 1 + i),),
+    )
+
+    def level_at(part, i):
+        return next(at(i) for begin, end, at in segments[part] if begin <= i < end)
+
+    def place_of(z):
+        if z in (0, levels - 1):
+            return 0, min(z, 1)
+        return (0, z + 1) if z < half - 1 else (1, z - half + 1)
+
     lane = lax.broadcasted_iota(jnp.int32, (8, 128), 1)
     wide_lane = lax.broadcasted_iota(jnp.int32, (CHUNK, 128), 1)
 
@@ -225,11 +239,10 @@
             axis=0,
         )
 
-    def put(k, part, z, r0, head, cond, keep_head=True):
+    def put(k, part, at0, z, r0, head, cond, keep_head=True):
         if keep_head:
             hp[k][z + 1, pl.ds(PAD + r0, CHUNK), :] = head
         kp[k][z + 1, pl.ds(PAD + r0, CHUNK), :] = cond
-        at0 = z - part * half
         if r0 == 0:
             xs[k, 0, part, 0, pl.ds(at0, 1), :] = head[0:1]
             xs[k, 0, part, 1, pl.ds(at0, 1), :] = cond[0:1]
@@ -297,8 +310,7 @@
     for load in loads[3:8]:
         load.wait()
 
-    def start_layer(part, i, c):
-        j = part * (layers // PARTS) + (layers // PARTS - 1 - i)
+    def start_layer(j):
         for r0 in range(0, rows, CHUNK):
             rs = pl.ds(r0, CHUNK)
             sum_s = None
@@ -313,7 +325,8 @@
                 m_v[z, rs, :] = m
                 sat, cond = curves(head, la, vn, m, ks_v[z, rs, :])
                 th_v[z, rs, :] = po_v[z, rs, :] * sat
-                put(0, part, z, r0, head, cond, keep_head=False)
+                part, at0 = place_of(z)
+                put(0, part, at0, z, r0, head, cond, keep_head=False)
                 sum_s = sat if sum_s is None else sum_s + sat
                 sum_h = head if sum_h is None else sum_h + head
             mean_h = sum_h * 0.25
@@ -325,9 +338,9 @@
                         piece * rows + r0 : piece * rows + r0 + CHUNK,
                         f * cols : (f + 1) * cols,
                     ] = value
-        return c
-
-    lax.fori_loop(0, layers // PARTS, functools.partial(start_layer, 0), 0)
+
+    start_layer(0)
+    start_layer(layers - 1)
 
     pl.semaphore_wait(barrier, (n_gx - 1) + (n_gz - 1) + 2)
 
@@ -357,9 +370,10 @@
     lax.fori_loop(1, n_gx, zt_start, 0)
     rt_v[gx, gz] = tp_v[gx]
 
-    send(face_z(0, 0) + faces_xy(0, 0))
-    lax.fori_loop(0, layers // PARTS, functools.partial(start_layer, 1), 0)
-    send(face_z(0, 1) + faces_xy(0, 1))
+    send(face_z(0, 0) + face_z(0, 1))
+    for j in range(1, layers - 1):
+        start_layer(j)
+        send(faces_xy(0, j - 1) if layers - 2 == PARTS else [])
 
     for j in range(layers):
         out = jnp.dot(sel_v[...], mean_v[j], preferred_element_type=jnp.float32)
@@ -370,9 +384,9 @@
     ]
     pl.semaphore_wait(line_sem, n_gz - 1)
 
-    def land_start(i, c):
-        to_gx = lax.rem(gx + i // n_gz, n_gx)
-        to_gz = lax.rem(gz + lax.rem(i, n_gz), n_gz)
+    def land_copy(off_gx, off_gz):
+        to_gx = lax.rem(gx + off_gx, n_gx)
+        to_gz = lax.rem(gz + off_gz, n_gz)
         to = to_gx * n_gz + to_gz
         pltpu.make_async_remote_copy(
             src_ref=tx_v.at[pl.ds(pl.multiple_of(to * per, 8), per), :],
@@ -382,11 +396,27 @@
             device_id={"gx": to_gx, "gz": to_gz},
             device_id_type=MESH,
         ).start()
-        return c
-
-    cut1 = groups // 4
-    cut2 = groups // 2
-    lax.fori_loop(1, cut1, land_start, 0)
+
+    n_across = n_gx * (n_gz - 1)
+    n_land = groups - 1
+
+    def land_across(i, c):
+        land_copy(i // (n_gz - 1), 1 + lax.rem(i, n_gz - 1))
+        return c
+
+    def land_along(i, c):
+        land_copy(1 + i - n_across, 0)
+        return c
+
+    def land_starts(begin, end):
+        if begin < min(end, n_across):
+            lax.fori_loop(begin, min(end, n_across), land_across, 0)
+        if max(begin, n_across) < end:
+            lax.fori_loop(max(begin, n_across), end, land_along, 0)
+
+    at1 = PACE[0] * groups // 64
+    at2 = at1 + PACE[1] * groups // 64
+    land_starts(0, at1)
 
     def drain(ref, count, sem):
         pltpu.make_async_copy(ref.at[pl.ds(0, count)], ref.at[pl.ds(0, count)], sem).wait()
@@ -405,22 +435,27 @@
 
     for i in range(1, n_gz):
         xt_copy(i).start()
+    land_starts(at1, at2)
 
     sign = jnp.where(jnp.bitwise_and(lane, 15) < half, 1.0, -1.0)
 
     def wait_part(k, part):
         views = [(2 * part + d, xh.at[k, d, part]) for d in range(2)]
         views += [(4 + 2 * part + d, yh.at[k, d, part]) for d in range(2)]
-        plane, edge = (0, 1) if part == 0 else (levels + 1, levels)
-        for f, ref in enumerate((hp[k], kp[k])):
-            views.append((8 + 2 * f + part, ref.at[plane, pl.ds(PAD, rows), :]))
+        if part == 0:
+            for d, plane in enumerate((0, levels + 1)):
+                for f, ref in enumerate((hp[k], kp[k])):
+                    views.append((8 + 2 * f + d, ref.at[plane, pl.ds(PAD, rows), :]))
         for slot, view in views:
             pltpu.make_async_copy(view, view, h_recv.at[k * 12 + slot]).wait()
 
-        @pl.when(gz == (0 if part == 0 else n_gz - 1))
-        def _():
-            hp[k][plane, pl.ds(PAD, rows), :] = hp[k][edge, pl.ds(PAD, rows), :]
-            kp[k][plane, pl.ds(PAD, rows), :] = -kp[k][edge, pl.ds(PAD, rows), :]
+        if part == 0:
+            for plane, edge, at_end in ((0, 1, 0), (levels + 1, levels, n_gz - 1)):
+
+                @pl.when(gz == at_end)
+                def _():
+                    hp[k][plane, pl.ds(PAD, rows), :] = hp[k][edge, pl.ds(PAD, rows), :]
+                    kp[k][plane, pl.ds(PAD, rows), :] = -kp[k][edge, pl.ds(PAD, rows), :]
 
         for d in range(2):
 
@@ -436,14 +471,13 @@
         for d, row in ((0, PAD - 1), (1, PAD + rows)):
             for f, ref in enumerate((hp[k], kp[k])):
                 for i in range(half):
-                    z = part * half + i
+                    z = level_at(part, i)
                     ref[z + 1, row : row + 1, :] = xh[k, d, part, f, i : i + 1, :]
 
-    def stencil(k, part, z, r0):
+    def stencil(k, part, at0, z, r0):
         def cut(ref, plane, shift):
             return ref[k][plane, pl.ds(PAD + r0 + shift, CHUNK), :]
 
-        at0 = z - part * half
         h, c = cut(hp, z + 1, 0), cut(kp, z + 1, 0)
         first, last = wide_lane == 0, wide_lane == 127
         c_ym = jnp.where(first, take_y(k, 0, part, r0, at0, 1), pltpu.roll(c, 1, 1))
@@ -463,18 +497,18 @@
         diag = 2.0 + ((kf_up + kf_dn) + (kf_xm + kf_xp) + (kf_ym + kf_yp))
         return h, flux + (c_dn - c_up), diag
 
-    def first_half(part, i, c):
-        z = part * half + (half - 1 - i)
+    def first_half(part, level, i, c):
+        z = level(i)
         for r0 in range(0, rows, CHUNK):
-            _, resid, diag = stencil(0, part, z, r0)
+            _, resid, diag = stencil(0, part, i, z, r0)
             ra_v[z, pl.ds(r0, CHUNK), :] = resid
             da_v[z, pl.ds(r0, CHUNK), :] = OMEGAS[0] / diag
         return c
 
     for part in range(PARTS):
         wait_part(0, part)
-        lax.fori_loop(0, half, functools.partial(first_half, part), 0)
-    lax.fori_loop(cut1, cut2, land_start, 0)
+        for begin, end, level in segments[part]:
+            lax.fori_loop(begin, end, functools.partial(first_half, part, level), 0, unroll=2)
 
     ref3 = rt_v.at[:, pl.ds(0, n_gz - 1)]
     pltpu.make_async_copy(ref3, ref3, xt_recv).wait()
@@ -504,44 +538,48 @@
             stress = 1.0 / (1.0 + lh * lh * (1.0 / 2.25))
             sk_v[j, rs, :] = 2.0 * (scale * (weight / total) * stress)
 
-    def curve_into(k, part, z, r0, head):
+    def curve_into(k, part, at0, z, r0, head):
         rs = pl.ds(r0, CHUNK)
         sat, cond = curves(head, la_v[z, rs, :], vn_v[z, rs, :], m_v[z, rs, :], ks_v[z, rs, :])
-        put(k, part, z, r0, head, cond)
+        put(k, part, at0, z, r0, head, cond)
         gain = po_v[z, rs, :] * sat - th_v[z, rs, :]
         ra_v[z, rs, :] = (gain + gain) + sk_v[z // LEVELS_PER_LAYER, rs, :]
 
-    def second_half(part, i, c):
-        z = part * half + (half - 1 - i)
+    def second_half(part, level, i, c):
+        z = level(i)
         for r0 in range(0, rows, CHUNK):
             rs = pl.ds(r0, CHUNK)
             resid = ra_v[z, rs, :] + sk_v[z // LEVELS_PER_LAYER, rs, :]
             head = hp[0][z + 1, pl.ds(PAD + r0, CHUNK), :]
-            curve_into(1, part, z, r0, head - resid * da_v[z, rs, :])
-        return c
-
-    def sweep_level(k, part, i, c):
-        z = part * half + (half - 1 - i)
+            curve_into(1, part, i, z, r0, head - resid * da_v[z, rs, :])
+        return c
+
+    def sweep_level(k, part, level, i, c):
+        z = level(i)
         for r0 in range(0, rows, CHUNK):
             rs = pl.ds(r0, CHUNK)
-            head, flux, diag = stencil(k, part, z, r0)
+            head, flux, diag = stencil(k, part, i, z, r0)
             head = head - (ra_v[z, rs, :] + flux) * (OMEGAS[k] / diag)
             if k + 1 < SWEEPS:
-                curve_into(k + 1, part, z, r0, head)
+                curve_into(k + 1, part, i, z, r0, head)
             else:
                 out_p[z, rs, :] = head
         return c
 
+    def run(k, part, body):
+        for begin, end, level in segments[part]:
+            lax.fori_loop(begin, end, functools.partial(body, part, level), 0, unroll=2)
+            if k < SWEEPS and part == 0 and begin == 0:
+                send(face_z(k, 0) + face_z(k, 1))
+        if k < SWEEPS:
+            send(faces_xy(k, part))
+
     for part in range(PARTS):
-        lax.fori_loop(0, half, functools.partial(second_half, part), 0)
-        send(face_z(1, part) + faces_xy(1, part))
-    lax.fori_loop(cut2, groups, land_start, 0)
-    for k in range(1, SWEEPS):
-        for part in range(PARTS):
-            wait_part(k, part)
-            lax.fori_loop(0, half, functools.partial(sweep_level, k, part), 0)
-            if k + 1 < SWEEPS:
-                send(face_z(k + 1, part) + faces_xy(k + 1, part))
+        run(1, part, second_half)
+    land_starts(at2, n_land)
+    for part in range(PARTS):
+        wait_part(1, part)
+        run(2, part, functools.partial(sweep_level, 1))
 
     for load in loads[8:]:
         load.wait()
@@ -592,6 +630,10 @@
                 out_lt[pl.ds((b0 * CAP + r) * n_layers + d, sub, stride=CAP * n_layers), :] = (
                     jnp.where(filled, temps[d], old[d])
                 )
+
+    for part in range(PARTS):
+        wait_part(2, part)
+        run(3, part, functools.partial(sweep_level, 2))
 
     for copy in started:
         copy.wait_send()

time: 49.4 us -> 40.7 us (0.82)
  Pallas kernels: 45.9 us -> 36.8 us
    pallas_call x1, Pallas kernels: 45.9 us -> 36.8 us  [local(): pl.pallas_call(functools.partial(kernel, n_role, n_gx, n_gz), out_shape=(...]
where the time goes in v3:
time: 40.7 us; the launch traced here: 40.2 us
  Pallas kernels  36.8 us (90%)
  local copies, waits for them, and re-layouts  2.68 us (7%)
  between operations  0.65 us (2%)
    pallas_call x1, Pallas kernels, local(): pl.pallas_call(functools.partial(kernel, n_role, n_gx, n_gz), out_shape=(...  36.8 us
    unnamed x4, local copies, waits for them, and re-layouts  2.68 us

profile of v3, /device:TPU:1, one launch (start us, length us, event | category | flops | bytes accessed | tf_op | source)
XLA Modules:
  0.0 40.2 jit_solution(15700257497623938324)
XLA Ops:
  0.6 36.8 %shard_map.113 = (f32[16,64,128]{2,1,0:T(8,128)}, f32[768,128]{1,0:T(8,128)}) custom-call(f32[16,64,128]{2,1,0:T(8,128)} %p_hbm.1, f32[16,64,128]{2,1,0:T(8,128)} %al_hbm.1, f32[16,64,128]{2,1,0:T(8,128)} %vn_hbm.1, f32[16,64,128]{2,1,0:T(8,128)} %ks_hbm.1, f32[16,64,128]{2,1,0:T(8,128)} %po_hbm.1, s32[4,1024]{1,0:T(4,128)} %bitcast.11, f32[768,128]{1,0:T(8,128)} %bitcast.6, ...), custom_call_target="tpu_custom_call" | custom-call | tf_op jit(solution)/shard_map/pallas_call | solution.py:662
  37.5 0.0 copy-start
  37.5 1.9 %copy.14 = f32[16,64,128]{2,1,0:T(8,128)} copy(f32[16,64,128]{2,1,0:T(8,128)} %get-tuple-element.8) | data formatting | bytes 1048576
  39.4 0.0 copy-done
  39.4 0.7 %copy.15 = f32[1,1,48,16,128]{4,3,2,1,0:T(8,128)} copy(f32[1,1,48,16,128]{4,3,2,1,0:T(8,128)S(1)} %bitcast.7) | data formatting | bytes 786432
Async XLA Ops:
  37.5 1.9 %copy-start = (f32[768,128]{1,0:T(8,128)S(1)}, f32[768,128]{1,0:T(8,128)}, u32[]{:S(2)}) copy-start(f32[768,128]{1,0:T(8,128)} %get-tuple-element.5) | copy-start | bytes 1179652

commit v4 on v3

--- a/solution.py
+++ b/solution.py
@@ -342,6 +342,16 @@
     start_layer(0)
     start_layer(layers - 1)
 
+    for j in range(1, layers - 1):
+        start_layer(j)
+
+    for j in range(layers):
+        out = jnp.dot(sel_v[...], mean_v[j], preferred_element_type=jnp.float32)
+        tx_v[pl.ds(j, groups * CAP, stride=tile), :] = out[:, :cols]
+        tx_v[pl.ds(layers + j, groups * CAP, stride=tile), :] = out[:, cols:]
+    rx_v[pl.ds(pl.multiple_of(me * per, 8), per), :] = tx_v[
+        pl.ds(pl.multiple_of(me * per, 8), per), :
+    ]
     pl.semaphore_wait(barrier, (n_gx - 1) + (n_gz - 1) + 2)
 
     def tell_line(i, c):
@@ -371,17 +381,9 @@
     rt_v[gx, gz] = tp_v[gx]
 
     send(face_z(0, 0) + face_z(0, 1))
-    for j in range(1, layers - 1):
-        start_layer(j)
-        send(faces_xy(0, j - 1) if layers - 2 == PARTS else [])
-
-    for j in range(layers):
-        out = jnp.dot(sel_v[...], mean_v[j], preferred_element_type=jnp.float32)
-        tx_v[pl.ds(j, groups * CAP, stride=tile), :] = out[:, :cols]
-        tx_v[pl.ds(layers + j, groups * CAP, stride=tile), :] = out[:, cols:]
-    rx_v[pl.ds(pl.multiple_of(me * per, 8), per), :] = tx_v[
-        pl.ds(pl.multiple_of(me * per, 8), per), :
-    ]
+    for part in range(PARTS):
+        send(faces_xy(0, part))
+
     pl.semaphore_wait(line_sem, n_gz - 1)
 
     def land_copy(off_gx, off_gz):
@@ -665,7 +667,7 @@
                 jax.ShapeDtypeStruct(p.shape, f32),
                 jax.ShapeDtypeStruct((slots * n_layers, cols), f32),
             ),
-            in_specs=[pl.BlockSpec(memory_space=pl.ANY)] * 10,
+            in_specs=[pl.BlockSpec(memory_space=pltpu.HBM)] * 10,
             out_specs=[pl.BlockSpec(memory_space=pltpu.VMEM)] * 2,
             scratch_shapes=[
                 cell,
@@ -716,19 +718,24 @@
                 pltpu.SemaphoreType.REGULAR,
             ],
             compiler_params=pltpu.CompilerParams(
-                collective_id=0, has_side_effects=True, vmem_limit_bytes=56 * 1024 * 1024
+                collective_id=0, has_side_effects=True, vmem_limit_bytes=28 * 1024 * 1024
             ),
         )(
-            p,
-            al,
-            vn,
-            ks,
-            po,
-            owner.T,
-            land.reshape(slots * n_layers, cols),
-            transp.reshape(slots, cols),
-            air.reshape(slots, cols),
-            roots.reshape(slots, cols),
+            *[
+                pltpu.with_memory_space_constraint(x, pltpu.HBM)
+                for x in (
+                    p,
+                    al,
+                    vn,
+                    ks,
+                    po,
+                    owner.T,
+                    land.reshape(slots * n_layers, cols),
+                    transp.reshape(slots, cols),
+                    air.reshape(slots, cols),
+                    roots.reshape(slots, cols),
+                )
+            ]
         )
         return head, temps.reshape(land.shape)
 

time: 40.7 us -> 38.4 us (0.943); the launches traced: 40.2 us -> 38.3 us
  local copies, waits for them, and re-layouts: 2.68 us -> 1.54 us
  Pallas kernels: 36.8 us -> 36.1 us
    unnamed x4 -> x2, local copies, waits for them, and re-layouts: 2.68 us -> 1.54 us
    pallas_call x1, Pallas kernels: 36.8 us -> 36.1 us  [local(): pl.pallas_call(functools.partial(kernel, n_role, n_gx, n_gz), out_shape=(...]
where the time goes in v4:
time: 38.4 us; the launch traced here: 38.3 us
  Pallas kernels  36.1 us (94%)
  local copies, waits for them, and re-layouts  1.54 us (4%)
  between operations  0.64 us (2%)
    pallas_call x1, Pallas kernels, local(): pl.pallas_call(functools.partial(kernel, n_role, n_gx, n_gz), out_shape=(...  36.1 us
    unnamed x2, local copies, waits for them, and re-layouts  1.54 us

profile of v4, /device:TPU:1, one launch (start us, length us, event | category | flops | bytes accessed | tf_op | source)
XLA Modules:
  0.0 38.3 jit_solution(1891805035254191847)
XLA Ops:
  0.6 36.1 %shard_map.113 = (f32[16,64,128]{2,1,0:T(8,128)S(1)}, f32[768,128]{1,0:T(8,128)S(1)}) custom-call(f32[16,64,128]{2,1,0:T(8,128)} %p_hbm.1, f32[16,64,128]{2,1,0:T(8,128)} %al_hbm.1, f32[16,64,128]{2,1,0:T(8,128)} %vn_hbm.1, f32[16,64,128]{2,1,0:T(8,128)} %ks_hbm.1, f32[16,64,128]{2,1,0:T(8,128)} %po_hbm.1, s32[4,1024]{1,0:T(4,128)} %bitcast.11, ...), custom_call_target="tpu_custom_call" | custom-call | tf_op jit(solution)/shard_map/pallas_call | solution.py:664
  36.8 0.8 %copy.14 = f32[16,64,128]{2,1,0:T(8,128)} copy(f32[16,64,128]{2,1,0:T(8,128)S(1)} %get-tuple-element.8) | data formatting | bytes 1048576
  37.6 0.7 %copy.15 = f32[1,1,48,16,128]{4,3,2,1,0:T(8,128)} copy(f32[1,1,48,16,128]{4,3,2,1,0:T(8,128)S(1)} %bitcast.6) | data formatting | bytes 786432

commit v5 on v4

--- a/solution.py
+++ b/solution.py
@@ -114,27 +114,6 @@
     kp = (kp0, kp1, kp2)
     half = levels // PARTS
 
-    barrier = pltpu.get_barrier_semaphore()
-
-    def greet_gx(i, c):
-        pl.semaphore_signal(
-            barrier, inc=1, device_id={"gx": lax.rem(gx + i, n_gx)}, device_id_type=MESH
-        )
-        return c
-
-    def greet_gz(i, c):
-        pl.semaphore_signal(
-            barrier, inc=1, device_id={"gz": lax.rem(gz + i, n_gz)}, device_id_type=MESH
-        )
-        return c
-
-    lax.fori_loop(1, n_gx, greet_gx, 0)
-    lax.fori_loop(1, n_gz, greet_gz, 0)
-    for step in (1, n_role - 1):
-        pl.semaphore_signal(
-            barrier, inc=1, device_id={"role": lax.rem(role + step, n_role)}, device_id_type=MESH
-        )
-
     pairs = (
         (tr_hbm, tr_v),
         (ro_hbm, ro_v),
@@ -150,6 +129,27 @@
     loads = [pltpu.make_async_copy(a, b, load_sem.at[i]) for i, (a, b) in enumerate(pairs)]
     for load in loads:
         load.start()
+
+    barrier = pltpu.get_barrier_semaphore()
+
+    def greet_gx(i, c):
+        pl.semaphore_signal(
+            barrier, inc=1, device_id={"gx": lax.rem(gx + i, n_gx)}, device_id_type=MESH
+        )
+        return c
+
+    def greet_gz(i, c):
+        pl.semaphore_signal(
+            barrier, inc=1, device_id={"gz": lax.rem(gz + i, n_gz)}, device_id_type=MESH
+        )
+        return c
+
+    lax.fori_loop(1, n_gx, greet_gx, 0)
+    lax.fori_loop(1, n_gz, greet_gz, 0)
+    for step in (1, n_role - 1):
+        pl.semaphore_signal(
+            barrier, inc=1, device_id={"role": lax.rem(role + step, n_role)}, device_id_type=MESH
+        )
 
     loads[0].wait()
     loads[1].wait()
@@ -384,7 +384,6 @@
     for part in range(PARTS):
         send(faces_xy(0, part))
 
-    pl.semaphore_wait(line_sem, n_gz - 1)
 
     def land_copy(off_gx, off_gz):
         to_gx = lax.rem(gx + off_gx, n_gx)
@@ -402,12 +401,16 @@
     n_across = n_gx * (n_gz - 1)
     n_land = groups - 1
 
+    def far_first(i):
+        step = (i + 1) // 2
+        return n_gx // 2 + step * (1 - 2 * lax.rem(i + 1, 2))
+
     def land_across(i, c):
         land_copy(i // (n_gz - 1), 1 + lax.rem(i, n_gz - 1))
         return c
 
     def land_along(i, c):
-        land_copy(1 + i - n_across, 0)
+        land_copy(far_first(i - n_across), 0)
         return c
 
     def land_starts(begin, end):
@@ -418,6 +421,9 @@
 
     at1 = PACE[0] * groups // 64
     at2 = at1 + PACE[1] * groups // 64
+    first = n_land - 3 * groups // 64
+    land_starts(first, n_land)
+    pl.semaphore_wait(line_sem, n_gz - 1)
     land_starts(0, at1)
 
     def drain(ref, count, sem):
@@ -578,7 +584,7 @@
 
     for part in range(PARTS):
         run(1, part, second_half)
-    land_starts(at2, n_land)
+    land_starts(at2, first)
     for part in range(PARTS):
         wait_part(1, part)
         run(2, part, functools.partial(sweep_level, 1))

time: 38.4 us -> 38.2 us (level)
  no operation moved by 1% of the time
where the time goes in v5:
time: 38.2 us; the launch traced here: 38.1 us
  Pallas kernels  35.9 us (94%)
  local copies, waits for them, and re-layouts  1.54 us (4%)
  between operations  0.64 us (2%)
    pallas_call x1, Pallas kernels, local(): pl.pallas_call(functools.partial(kernel, n_role, n_gx, n_gz), out_shape=(...  35.9 us
    unnamed x2, local copies, waits for them, and re-layouts  1.54 us

profile of v5, /device:TPU:1, one launch (start us, length us, event | category | flops | bytes accessed | tf_op | source)
XLA Modules:
  0.0 38.1 jit_solution(17083089177169981503)
XLA Ops:
  0.6 35.9 %shard_map.113 = (f32[16,64,128]{2,1,0:T(8,128)S(1)}, f32[768,128]{1,0:T(8,128)S(1)}) custom-call(f32[16,64,128]{2,1,0:T(8,128)} %p_hbm.1, f32[16,64,128]{2,1,0:T(8,128)} %al_hbm.1, f32[16,64,128]{2,1,0:T(8,128)} %vn_hbm.1, f32[16,64,128]{2,1,0:T(8,128)} %ks_hbm.1, f32[16,64,128]{2,1,0:T(8,128)} %po_hbm.1, s32[4,1024]{1,0:T(4,128)} %bitcast.11, ...), custom_call_target="tpu_custom_call" | custom-call | tf_op jit(solution)/shard_map/pallas_call | solution.py:670
  36.6 0.8 %copy.14 = f32[16,64,128]{2,1,0:T(8,128)} copy(f32[16,64,128]{2,1,0:T(8,128)S(1)} %get-tuple-element.8) | data formatting | bytes 1048576
  37.4 0.7 %copy.15 = f32[1,1,48,16,128]{4,3,2,1,0:T(8,128)} copy(f32[1,1,48,16,128]{4,3,2,1,0:T(8,128)S(1)} %bitcast.6) | data formatting | bytes 786432
